TPU v7x, 128 devices: a whole 4x4x4 slice. The times are simulated.
128 devices in a mesh: tok: 32 (over y, x, core), mlp: 4 (over z).
Axes of the slice: x: 4, y: 4, z: 4, core: 2. Of those that a mesh axis runs over, the one named last changes fastest.
Arguments:
- layer_input: bfloat16 [16384, 4096], P('tok'), may hold values from -80 to 80
- input_norm_gain: float32 [4096], replicated, may hold values from 0.6 to 10
- query_weight: bfloat16 [4096, 4096], P(None, 'mlp'), may hold values from -0.09375 to 0.09375
- key_weight: bfloat16 [4096, 1024], P(None, 'mlp'), may hold values from -0.09375 to 0.09375
- value_weight: bfloat16 [4096, 1024], P(None, 'mlp'), may hold values from -0.09375 to 0.09375
- query_down_maps: bfloat16 [256, 16, 4096], P('tok', None, 'mlp'), may hold values from -0.09375 to 0.09375
- value_down_maps: bfloat16 [256, 16, 4096], P('tok', None, 'mlp'), may hold values from -0.09375 to 0.09375
- query_up_maps: bfloat16 [256, 16, 4096], P('tok', None, 'mlp'), may hold values from -1.5 to 1.5
- value_up_maps: bfloat16 [256, 16, 1024], P('tok', None, 'mlp'), may hold values from -1.5 to 1.5
- tenant_prompt_length: int32 [16], replicated, may hold values from 1 to 2048, 16384 in all
- tenant_adapter_id: int32 [16], replicated, may hold values from 0 to 255
- adapter_storage_slot: int32 [256], replicated, may hold values from 0 to 255, each once
Outputs:
- attended: bfloat16 [16384, 4096], P('tok', 'mlp')
Inputs may be any that keep to these rules, and one draw needn't show every extreme that they name: `tenant_prompt_length`: the lengths sum to 16384; each is at most 2048 and one of them is exactly that. `tenant_adapter_id`: tenants may share an adapter. `adapter_storage_slot`: each storage slot holds exactly one adapter.
All inputs are finite; a program needn't handle non-finite values.
Results may differ from a plain program's by a relative error of at most 0.0045.
The roundings to bfloat16 on the way count: a program that leaves them out, or rounds other values in their place, can miss the bound.
Values may be sent and summed in bfloat16 or wider, within the bound.
A program may use at most 192 MiB of HBM per device.

v0:
```python
import jax
import jax.numpy as jnp
from jax import lax
from jax.sharding import PartitionSpec as P

HEAD_WIDTH = 128
ADAPTER_RANK = 16
LONGEST_PROMPT = 4


NORM_EPS = 1e-05
ROPE_BASE = 500000.0
ADAPTER_SCALE = 0.5


def from_behind(x, axis, by):
    peers = lax.axis_size(axis)
    pairs = [(i, i + by) for i in range(peers) if 0 <= i + by < peers]
    return lax.ppermute(x, axis, pairs)


def rotary(values, positions):
    half_width = values.shape[-1] // 2
    exponent = jnp.arange(half_width).astype(jnp.float32) * (2.0 / values.shape[-1])
    inverse = jnp.exp(-exponent * jnp.log(jnp.float32(ROPE_BASE)))
    angles = positions.astype(jnp.float32)[:, None] * inverse[None, :]
    cosine = jnp.cos(angles)[:, None, :]
    sine = jnp.sin(angles)[:, None, :]
    first_position = values[..., :half_width]
    second = values[..., half_width:]
    return jnp.concatenate(
        [first_position * cosine - second * sine, second * cosine + first_position * sine], axis=-1
    )


def tenant_of(tenant_prompt_length, indices):
    prompt_ends = jnp.cumsum(tenant_prompt_length)
    prompt_starts = prompt_ends - tenant_prompt_length
    tenant_ids = jnp.sum((indices[:, None] >= prompt_ends[None, :]).astype(jnp.int32), axis=1)
    member = (
        tenant_ids[:, None] == jnp.arange(tenant_prompt_length.shape[0], dtype=jnp.int32)[None, :]
    )
    row_start = jnp.sum(jnp.where(member, prompt_starts[None, :], 0), axis=1)
    return (member, row_start)


def contract(left, table):
    flat = table.reshape(-1, table.shape[2])
    return lax.dot_general(left, flat, (((1,), (1,)), ((), ())), preferred_element_type=jnp.float32)


def body(
    layer_input,
    input_norm_gain,
    query_weight,
    key_weight,
    value_weight,
    query_down_maps,
    value_down_maps,
    query_up_maps,
    value_up_maps,
    tenant_prompt_length,
    tenant_adapter_id,
    adapter_storage_slot,
):
    tok_rows = layer_input.shape[0]
    device = lax.axis_index("tok")
    held_tokens = query_down_maps.shape[0]
    catalog = adapter_storage_slot.shape[0]
    matches = tenant_adapter_id[:, None] == jnp.arange(catalog, dtype=jnp.int32)[None, :]
    storage_slots = jnp.sum(jnp.where(matches, adapter_storage_slot[None, :], 0), axis=1)
    local_slot = storage_slots - device * held_tokens
    picker = (local_slot[:, None] == jnp.arange(held_tokens, dtype=jnp.int32)[None, :]).astype(
        jnp.bfloat16
    )

    def selector(stored):
        return jnp.einsum("th,hrc->trc", picker, stored, preferred_element_type=jnp.float32)

    summed = (
        lax.psum(selector(query_down_maps).astype(jnp.bfloat16), "tok").astype(jnp.float32),
        lax.psum(selector(value_down_maps).astype(jnp.bfloat16), "tok").astype(jnp.float32),
        lax.psum(selector(query_up_maps).astype(jnp.bfloat16), "tok").astype(jnp.float32),
        lax.psum(selector(value_up_maps).astype(jnp.bfloat16), "tok").astype(jnp.float32),
    )
    query_down_table = summed[0].astype(jnp.bfloat16)
    value_down_table = summed[1].astype(jnp.bfloat16)
    query_up_table = summed[2].astype(jnp.bfloat16)
    value_up_table = summed[3].astype(jnp.bfloat16)
    widened = layer_input.astype(jnp.float32)
    scale_row = lax.rsqrt(jnp.mean(widened * widened, axis=1, keepdims=True) + NORM_EPS)
    normed_input = (widened * scale_row * input_norm_gain[None, :]).astype(jnp.bfloat16)
    indices = device * tok_rows + jnp.arange(tok_rows, dtype=jnp.int32)
    member, row_start = tenant_of(tenant_prompt_length, indices)
    positions = indices - row_start
    chosen = jnp.repeat(member, ADAPTER_RANK, axis=1)
    full_aq, full_av = (
        lax.all_gather(query_down_table, "mlp", axis=2, tiled=True),
        lax.all_gather(value_down_table, "mlp", axis=2, tiled=True),
    )
    shrink_q = contract(normed_input, full_aq)
    shrink_v = contract(normed_input, full_av)
    shrink_q = jnp.where(chosen, shrink_q, 0.0).astype(jnp.bfloat16)
    shrink_v = jnp.where(chosen, shrink_v, 0.0).astype(jnp.bfloat16)
    query_delta = jnp.dot(
        shrink_q,
        query_up_table.reshape(-1, query_up_table.shape[2]),
        preferred_element_type=jnp.float32,
    )
    value_delta = jnp.dot(
        shrink_v,
        value_up_table.reshape(-1, value_up_table.shape[2]),
        preferred_element_type=jnp.float32,
    )
    query_rows = (
        jnp.dot(normed_input, query_weight, preferred_element_type=jnp.float32)
        + ADAPTER_SCALE * query_delta
    )
    query_rows = rotary(query_rows.reshape(tok_rows, -1, HEAD_WIDTH), positions).astype(
        jnp.bfloat16
    )
    key = jnp.dot(normed_input, key_weight, preferred_element_type=jnp.float32)
    key = rotary(key.reshape(tok_rows, -1, HEAD_WIDTH), positions).astype(jnp.bfloat16)
    value_rows = (
        jnp.dot(normed_input, value_weight, preferred_element_type=jnp.float32)
        + ADAPTER_SCALE * value_delta
    )
    value_rows = value_rows.astype(jnp.bfloat16).reshape(tok_rows, -1, HEAD_WIDTH)
    key_blocks = []
    value_blocks = []
    for shift_by in range(LONGEST_PROMPT, 0, -1):
        moved_key, moved_value = from_behind((key, value_rows), "tok", shift_by)
        key_blocks.append(moved_key)
        value_blocks.append(moved_value)
    key_blocks.append(key)
    value_blocks.append(value_rows)
    all_values = jnp.concatenate(value_blocks, axis=0)
    span = (LONGEST_PROMPT + 1) * tok_rows
    k_index = (device - LONGEST_PROMPT) * tok_rows + jnp.arange(span, dtype=jnp.int32)
    allowed = (k_index[None, :] >= row_start[:, None]) & (k_index[None, :] <= indices[:, None])
    heads_here = query_rows.shape[1]
    kv_here = key.shape[1]
    head_groups = heads_here // kv_here
    outputs = []
    for kv_group in range(kv_here):
        q_group = query_rows[:, kv_group * head_groups : (kv_group + 1) * head_groups, :]
        pieces = []
        for block_index in range(LONGEST_PROMPT + 1):
            block_keys = key_blocks[block_index][:, kv_group, :]

            def dense_scores(q_group=q_group, block_keys=block_keys):
                return jnp.einsum(
                    "qgd,kd->gqk", q_group, block_keys, preferred_element_type=jnp.float32
                )

            pieces.append(dense_scores())
        scores = jnp.concatenate(pieces, axis=2) * HEAD_WIDTH ** (-0.5)
        scores = jnp.where(allowed[None], scores, -jnp.inf)
        peak = jnp.max(scores, axis=-1, keepdims=True)
        weights = jnp.exp(scores - peak)
        totals = jnp.sum(weights, axis=-1)
        probs = weights.astype(jnp.bfloat16)
        mixed = jnp.einsum(
            "gqk,kd->qgd", probs, all_values[:, kv_group, :], preferred_element_type=jnp.float32
        )
        outputs.append(mixed / jnp.transpose(totals)[:, :, None])
    attended = jnp.concatenate(outputs, axis=1).astype(jnp.bfloat16)
    return attended.reshape(tok_rows, heads_here * HEAD_WIDTH)


def solution(mesh):
    placed = (
        P("tok", None),
        P(),
        P(None, "mlp"),
        P(None, "mlp"),
        P(None, "mlp"),
        P("tok", None, "mlp"),
        P("tok", None, "mlp"),
        P("tok", None, "mlp"),
        P("tok", None, "mlp"),
        P(),
        P(),
        P(),
    )
    return jax.shard_map(
        body, mesh=mesh, in_specs=placed, out_specs=P("tok", "mlp"), check_vma=False
    )
```

profile of v0, /device:TPU:1, one launch (start us, length us, event | category | flops | bytes accessed | tf_op | source)
XLA Modules:
  0.0 289.7 jit_solution(7563186682735671526)
XLA Ops:
  6.5 1.0 select_reduce_fusion.1
  7.6 1.1 convolution_convert_fusion.3
  8.6 0.7 copy.46
  9.3 1.3 convolution_convert_fusion
  10.6 1.1 copy.53
  11.7 2.1 convolution_convert_fusion.1
  13.8 2.1 convolution_convert_fusion.2
  16.0 0.0 all-gather.3.cloned.1.call-start
  16.0 0.1 copy.41
  16.1 0.1 reduce
  16.3 3.1 %fusion.12 = f32[512]{0:T(512)S(1)} fusion(bf16[512,4096]{1,0:T(8,128)(2,1)} %param.12), kind=kLoop, calls=%fused_computation.16 | loop fusion | flops 6290944 | bytes 4196352 | tf_op jit(solution)/shard_map/reduce_sum | solution.py:91
  19.4 106.0 %all-reduce.3.cloned.1.call-done = (bf16[256,1024]{1,0:T(8,128)(2,1)}, bf16[16,16,1024]{2,0,1:T(8,128)(2,1)}, bf16[256,256]{1,0:T(8,128)(2,1)}, bf16[16,16,1024]{2,0,1:T(8,128)(2,1)}) async-done(((bf16[256,1024]{1,0:T(8,128)(2,1)}, bf16[16,16,1024]{2,0,1:T(8,128)(2,1)}, bf16[256,256]{1,0:T(8,128)(2,1)}, bf16[16,16,1024]{2,0,1:T(8,128)(2,1)}), (bf16[256,1024]{1,0:T(8,128)(2,1)}, ...) | async-done | bytes 1703952 | tf_op jit(solution)/shard_map/psum | solution.py:83
  125.5 3.8 %fusion.14 = bf16[512,4096]{1,0:T(8,128)(2,1)S(1)} fusion(bf16[512,4096]{1,0:T(8,128)(2,1)} %param.12, f32[4096]{0:T(1024)S(1)} %copy-done.15, f32[512]{0:T(512)S(1)} %add_rsqrt_fusion), kind=kLoop, calls=%fused_computation.18 | loop fusion | flops 8388608 | bytes 8407040 | tf_op jit(solution)/shard_map/convert_element_type | solution.py:92
  129.3 1.9 copy-done.2
  131.3 1.3 fusion.62
  132.6 0.2 copy.62
  132.8 0.2 copy.61
  133.1 0.1 convert_reduce_fusion
  133.1 0.1 select_reduce_fusion
  133.2 1.0 multiply_cosine_fusion
  134.3 0.1 subtract_convert_fusion.1
  134.4 0.7 copy-done.4
  135.1 0.9 pad_maximum_fusion.2
  136.0 3.1 %collective-permute-start.7 = (bf16[512,2,128]{2,0,1:T(8,128)(2,1)}, bf16[512,2,128]{2,0,1:T(8,128)(2,1)}, u32[]{:S(2)}, u32[]{:S(2)}) collective-permute-start(bf16[512,2,128]{2,0,1:T(8,128)(2,1)} %pad_maximum_fusion.2), channel_id=1, source_target_pairs={{0,4},{4,8},{8,12},{12,16},{16,20},{20,24},{24,28},{28,32},{32,36}... | collective-permute-start | bytes 786440 | tf_op jit(solution)/shard_map/ppermute | solution.py:19
  139.1 3.8 %collective-permute-start.6 = (bf16[512,2,128]{2,0,1:T(8,128)(2,1)}, bf16[512,2,128]{2,0,1:T(8,128)(2,1)}, u32[]{:S(2)}, u32[]{:S(2)}) collective-permute-start(bf16[512,2,128]{2,0,1:T(8,128)(2,1)} %pad_maximum_fusion.2), channel_id=1, source_target_pairs={{0,8},{4,12},{8,16},{12,20},{16,24},{20,28},{24,32},{28,36},{32,40... | collective-permute-start | bytes 786440 | tf_op jit(solution)/shard_map/ppermute | solution.py:19
  142.9 4.9 %collective-permute-start.5 = (bf16[512,2,128]{2,0,1:T(8,128)(2,1)}, bf16[512,2,128]{2,0,1:T(8,128)(2,1)}, u32[]{:S(2)}, u32[]{:S(2)}) collective-permute-start(bf16[512,2,128]{2,0,1:T(8,128)(2,1)} %pad_maximum_fusion.2), channel_id=1, source_target_pairs={{0,12},{4,16},{8,20},{12,24},{16,28},{20,32},{24,36},{28,40},{32,4... | collective-permute-start | bytes 786440 | tf_op jit(solution)/shard_map/ppermute | solution.py:19
  147.9 2.0 collective-permute-start.4
  149.9 0.2 copy.44
  150.2 5.1 %fusion.61 = f32[512,256]{0,1:T(8,128)} fusion(bf16[512,4096]{1,0:T(8,128)(2,1)} %copy-done.2, bf16[4096,256]{1,0:T(8,128)(2,1)} %param.16), kind=kOutput, calls=%fused_computation.114 | convolution fusion | flops 1073741824 | bytes 6815744 | tf_op jit(solution)/shard_map/dot_general | solution.py:125
  155.3 1.3 compare_and_fusion
  156.7 8.3 %fusion.63 = f32[512,1024]{1,0:T(8,128)} fusion(bf16[512,4096]{1,0:T(8,128)(2,1)S(1)} %copy-done.3, bf16[4096,1024]{1,0:T(8,128)(2,1)} %param.14), kind=kOutput, calls=%fused_computation.116 | convolution fusion | flops 4294967296 | bytes 14680064 | tf_op jit(solution)/shard_map/dot_general | solution.py:116
  165.0 2.7 copy.43
  167.7 4.9 %fusion.24 = bf16[512,256]{0,1:T(8,128)(2,1)} fusion(f32[512,256]{0,1:T(8,128)} %fusion.61, bf16[256,256]{1,0:T(8,128)(2,1)} %get-tuple-element.9, pred[512,256]{1,0:T(32,128)(4,1)S(1)} %copy.44, bf16[512,4096]{1,0:T(8,128)(2,1)} %copy-done.2, bf16[256,4096]{1,0:T(8,128)(2,1)S(1)} %bitcast.121), kind=kOutput, calls=%fused_computation.44 | convolution fusion | flops 1141506048 | bytes 7340032 | tf_op jit(solution)/shard_map/dot_general | solution.py:110
  172.6 3.3 %collective-permute-start.3 = (bf16[512,2,128]{0,2,1:T(8,128)(2,1)}, bf16[512,2,128]{0,2,1:T(8,128)(2,1)}, u32[]{:S(2)}, u32[]{:S(2)}) collective-permute-start(bf16[512,2,128]{0,2,1:T(8,128)(2,1)} %bitcast.126), channel_id=1, source_target_pairs={{0,4},{4,8},{8,12},{12,16},{16,20},{20,24},{24,28},{28,32},{32,36}... | collective-permute-start | bytes 786440 | tf_op jit(solution)/shard_map/ppermute | solution.py:19
  175.9 14.5 %all-gather.5.cloned.1.call-done = bf16[16,16,4096]{2,0,1:T(8,128)(2,1)} async-done(((bf16[16,16,1024]{2,0,1:T(8,128)(2,1)}), bf16[16,16,4096]{2,0,1:T(8,128)(2,1)}) %all-gather.5.cloned.1.call-update) | async-done | bytes 2097168 | tf_op jit(solution)/shard_map/all_gather | solution.py:98
  190.4 2.7 copy.50
  193.2 6.5 %add_bitcast_fusion = f32[64,8,8,128]{3,1,2,0:T(8,128)} fusion(f32[512,1024]{1,0:T(8,128)} %fusion.63, bf16[256,1024]{1,0:T(8,128)(2,1)} %get-tuple-element.7, pred[512,256]{1,0:T(32,128)(4,1)S(1)} %copy.44, bf16[512,4096]{1,0:T(8,128)(2,1)} %copy-done.2, bf16[256,4096]{1,0:T(8,128)(2,1)S(1)} %bitcast.119), kind=kOutput, calls=%fused_computation.32 | convolution fusion | flops 1343488000 | bytes 11141120 | tf_op jit(solution)/shard_map/dot_general | solution.py:105
  199.7 2.1 copy.65
  201.7 0.7 fusion.59
  202.4 0.3 copy-done.9
  202.7 0.1 copy-done.11
  202.7 0.8 subtract_convert_fusion
  203.6 0.6 fusion.29
  204.2 3.1 %collective-permute-start.2 = (bf16[512,2,128]{0,2,1:T(8,128)(2,1)S(1)}, bf16[512,2,128]{0,2,1:T(8,128)(2,1)S(1)}, u32[]{:S(2)}, u32[]{:S(2)}) collective-permute-start(bf16[512,2,128]{0,2,1:T(8,128)(2,1)S(1)} %bitcast.127), channel_id=1, source_target_pairs={{0,8},{4,12},{8,16},{12,20},{16,24},{20,28},{24,32},{28,36},{32,40... | collective-permute-start | bytes 786440 | tf_op jit(solution)/shard_map/ppermute | solution.py:19
  207.3 1.6 bitcast_dynamic-update-slice_fusion.9
  208.9 5.1 %collective-permute-start.1 = (bf16[512,2,128]{0,2,1:T(8,128)(2,1)S(1)}, bf16[512,2,128]{0,2,1:T(8,128)(2,1)S(1)}, u32[]{:S(2)}, u32[]{:S(2)}) collective-permute-start(bf16[512,2,128]{0,2,1:T(8,128)(2,1)S(1)} %bitcast.128), channel_id=1, source_target_pairs={{0,12},{4,16},{8,20},{12,24},{16,28},{20,32},{24,36},{28,40},{32,4... | collective-permute-start | bytes 786440 | tf_op jit(solution)/shard_map/ppermute | solution.py:19
  214.1 1.6 bitcast_dynamic-update-slice_fusion.8
  215.7 3.8 %collective-permute-start = (bf16[512,2,128]{0,2,1:T(8,128)(2,1)S(1)}, bf16[512,2,128]{0,2,1:T(8,128)(2,1)S(1)}, u32[]{:S(2)}, u32[]{:S(2)}) collective-permute-start(bf16[512,2,128]{0,2,1:T(8,128)(2,1)S(1)} %bitcast.129), channel_id=1, source_target_pairs={{0,16},{4,20},{8,24},{12,28},{16,32},{20,36},{24,40},{28,44},{32,4... | collective-permute-start | bytes 786440 | tf_op jit(solution)/shard_map/ppermute | solution.py:19
  219.5 1.6 bitcast_dynamic-update-slice_fusion.7
  221.2 1.6 bitcast_dynamic-update-slice_fusion.6
  222.8 0.8 bitcast_dynamic-update-slice_fusion.5
  223.5 3.6 %bitcast_dynamic-update-slice_fusion.4 = f32[4,512,2560]{1,2,0:T(8,128)} fusion(bf16[512,4,128]{2,0,1:T(8,128)(2,1)S(1)} %get-tuple-element.14, bf16[512,2,128]{2,0,1:T(8,128)(2,1)} %collective-permute-done.4), kind=kOutput, calls=%fused_computation.24 | convolution fusion | flops 268435456 | bytes 4849664 | tf_op jit(solution)/shard_map/qgd,kd->gqk/dot_general | solution.py:152
  227.1 3.6 %bitcast_dynamic-update-slice_fusion.3 = f32[4,512,2560]{1,2,0:T(8,128)} fusion(f32[4,512,2560]{1,2,0:T(8,128)} %bitcast_dynamic-update-slice_fusion.4, bf16[512,4,128]{2,0,1:T(8,128)(2,1)S(1)} %get-tuple-element.14, bf16[512,2,128]{2,0,1:T(8,128)(2,1)} %collective-permute-done.5), kind=kOutput, calls=%fused_computation.23 | convolution fusion | flops 268435456 | bytes 4849664 | tf_op jit(solution)/shard_map/qgd,kd->gqk/dot_general | solution.py:152
  230.8 3.6 %bitcast_dynamic-update-slice_fusion.2 = f32[4,512,2560]{1,2,0:T(8,128)} fusion(f32[4,512,2560]{1,2,0:T(8,128)} %bitcast_dynamic-update-slice_fusion.3, bf16[512,4,128]{2,0,1:T(8,128)(2,1)S(1)} %get-tuple-element.14, bf16[512,2,128]{2,0,1:T(8,128)(2,1)} %collective-permute-done.6), kind=kOutput, calls=%fused_computation.22 | convolution fusion | flops 268435456 | bytes 4849664 | tf_op jit(solution)/shard_map/qgd,kd->gqk/dot_general | solution.py:152
  234.4 3.7 %bitcast_dynamic-update-slice_fusion.1 = f32[4,512,2560]{1,2,0:T(8,128)} fusion(f32[4,512,2560]{1,2,0:T(8,128)} %bitcast_dynamic-update-slice_fusion.2, bf16[512,4,128]{2,0,1:T(8,128)(2,1)S(1)} %get-tuple-element.14, bf16[512,2,128]{2,0,1:T(8,128)(2,1)} %collective-permute-done.7), kind=kOutput, calls=%fused_computation.21 | convolution fusion | flops 268435456 | bytes 4849664 | tf_op jit(solution)/shard_map/qgd,kd->gqk/dot_general | solution.py:152
  238.1 2.7 bitcast_dynamic-update-slice_fusion
  240.8 3.0 %fusion = f32[4,512]{1,0:T(4,128)S(1)} fusion(f32[4,512,2560]{1,2,0:T(8,128)S(1)} %bitcast_dynamic-update-slice_fusion.5, pred[512,2560]{0,1:T(8,128)(4,1)S(1)} %compare_and_fusion), kind=kLoop, calls=%fused_computation.4 | loop fusion | flops 15726592 | bytes 22290432 | tf_op jit(solution)/shard_map/reduce_max | solution.py:159
  243.8 10.6 %fusion.2 = (f32[4,512]{1,0:T(4,128)S(1)}, f32[4,512]{1,0:T(4,128)S(1)}) fusion(f32[4,512,2560]{1,2,0:T(8,128)S(1)} %bitcast_dynamic-update-slice_fusion.5, f32[4,512]{1,0:T(4,128)S(1)} %fusion, pred[512,2560]{0,1:T(8,128)(4,1)S(1)} %compare_and_fusion, f32[4,512,2560]{1,2,0:T(8,128)} %bitcast_dynamic-update-slice_fusion), kind=kLoop, calls=%fused_computation.6 | loop fusion | flops 36696064 | bytes 43278336 | tf_op jit(solution)/shard_map/reduce_sum | solution.py:161
  254.5 9.5 %fusion.4 = f32[4,512]{1,0:T(4,128)S(1)} fusion(f32[4,512,2560]{1,2,0:T(8,128)} %bitcast_dynamic-update-slice_fusion, f32[4,512]{1,0:T(4,128)S(1)} %get-tuple-element.6, pred[512,2560]{0,1:T(8,128)(4,1)S(1)} %compare_and_fusion), kind=kLoop, calls=%fused_computation.8 | loop fusion | flops 20969472 | bytes 22298624 | tf_op jit(solution)/shard_map/reduce_sum | solution.py:161
  264.1 1.0 constant_dynamic-update-slice_fusion.1
  265.1 6.5 %divide_convert_fusion.1 = bf16[512,4,128]{0,2,1:T(8,128)(2,1)} fusion(f32[4,512,2560]{1,2,0:T(8,128)S(1)} %bitcast_dynamic-update-slice_fusion.5, f32[4,512]{1,0:T(4,128)S(1)} %fusion, pred[512,2560]{0,1:T(8,128)(4,1)S(1)} %compare_and_fusion, bf16[2560,2,128]{0,2,1:T(8,128)(2,1)S(1)} %constant_dynamic-update-slice_fusion, f32[512,4]{0,1:T(4,128)S(1)} %bitcast.132), kind=kOutput, calls=%fused_computation.50 | convolution fusion | flops 1363673088 | bytes 23478272 | tf_op jit(solution)/shard_map/gqk,kd->qgd/dot_general | solution.py:163
  271.6 10.2 %divide_convert_fusion = bf16[512,4,128]{0,2,1:T(8,128)(2,1)S(1)} fusion(f32[4,512,2560]{1,2,0:T(8,128)} %bitcast_dynamic-update-slice_fusion, f32[4,512]{1,0:T(4,128)S(1)} %get-tuple-element.6, pred[512,2560]{0,1:T(8,128)(4,1)S(1)} %compare_and_fusion, bf16[2560,2,128]{0,2,1:T(8,128)(2,1)} %copy-done.14, f32[512,4]{0,1:T(4,128)S(1)} %bitcast.131), kind=kOutput, calls=%fused_computation.49 | convolution fusion | flops 1363673088 | bytes 23478272 | tf_op jit(solution)/shard_map/gqk,kd->qgd/dot_general | solution.py:163
  281.8 0.1 pad_maximum_fusion
  281.9 1.3 copy.58
  (59 shorter events, 0.4 us)
Async XLA Ops:
  6.5 124.7 %copy-start = (bf16[4096,256]{1,0:T(8,128)(2,1)S(1)}, bf16[4096,256]{1,0:T(8,128)(2,1)}, u32[]{:S(2)}) copy-start(bf16[4096,256]{1,0:T(8,128)(2,1)} %param.15) | copy-start | bytes 6291460
  6.5 9.5 %copy-start.16 = (s32[16]{0:T(128)S(1)}, s32[16]{0:T(128)}, u32[]{:S(2)}) copy-start(s32[16]{0:T(128)} %param.21) | copy-start | bytes 196
  6.5 118.9 %all-reduce.3.cloned.1.call-start = ((), (), s32[]{:S(2)}) async-start(), calls=%async_computation.2 | async-start | bytes 3407872 | tf_op jit(solution)/shard_map/psum | solution.py:83
  11.7 113.7 %copy-start.15 = (f32[4096]{0:T(1024)S(1)}, f32[4096]{0:T(1024)}, u32[]{:S(2)}) copy-start(f32[4096]{0:T(1024)} %param.13) | copy-start | bytes 49156
  16.0 149.0 %all-gather.3.cloned.1.call-start = ((), (), s32[]{:S(2)}) async-start(), calls=%async_computation | async-start | bytes 2621440 | tf_op jit(solution)/shard_map/all_gather | solution.py:99
  125.4 65.0 %all-gather.5.cloned.1.call-start = ((), (), s32[]{:S(2)}) async-start(), calls=%async_computation.1 | async-start | bytes 2621440 | tf_op jit(solution)/shard_map/all_gather | solution.py:98
  129.3 1.9 copy-start.2
  134.2 4.9 %copy-start.8 = (f32[512,64]{1,0:T(8,128)}, f32[512,64]{1,0:T(8,128)S(1)}, u32[]{:S(2)}) copy-start(f32[512,64]{1,0:T(8,128)S(1)} %get-tuple-element.21) | copy-start | bytes 393220
  134.2 8.7 %copy-start.10 = (f32[512,64]{1,0:T(8,128)}, f32[512,64]{1,0:T(8,128)S(1)}, u32[]{:S(2)}) copy-start(f32[512,64]{1,0:T(8,128)S(1)} %get-tuple-element.22) | copy-start | bytes 393220
  134.4 0.7 copy-start.4
  134.4 1.6 copy-start.6
  136.0 85.1 %collective-permute-start.7 = (bf16[512,2,128]{2,0,1:T(8,128)(2,1)}, bf16[512,2,128]{2,0,1:T(8,128)(2,1)}, u32[]{:S(2)}, u32[]{:S(2)}) collective-permute-start(bf16[512,2,128]{2,0,1:T(8,128)(2,1)} %pad_maximum_fusion.2), channel_id=1, source_target_pairs={{0,4},{4,8},{8,12},{12,16},{16,20},{20,24},{24,28},{28,32},{32,36}... | collective-permute-start | bytes 786440 | tf_op jit(solution)/shard_map/ppermute | solution.py:19
  139.1 76.6 %collective-permute-start.6 = (bf16[512,2,128]{2,0,1:T(8,128)(2,1)}, bf16[512,2,128]{2,0,1:T(8,128)(2,1)}, u32[]{:S(2)}, u32[]{:S(2)}) collective-permute-start(bf16[512,2,128]{2,0,1:T(8,128)(2,1)} %pad_maximum_fusion.2), channel_id=1, source_target_pairs={{0,8},{4,12},{8,16},{12,20},{16,24},{20,28},{24,32},{28,36},{32,40... | collective-permute-start | bytes 786440 | tf_op jit(solution)/shard_map/ppermute | solution.py:19
  142.9 66.0 %collective-permute-start.5 = (bf16[512,2,128]{2,0,1:T(8,128)(2,1)}, bf16[512,2,128]{2,0,1:T(8,128)(2,1)}, u32[]{:S(2)}, u32[]{:S(2)}) collective-permute-start(bf16[512,2,128]{2,0,1:T(8,128)(2,1)} %pad_maximum_fusion.2), channel_id=1, source_target_pairs={{0,12},{4,16},{8,20},{12,24},{16,28},{20,32},{24,36},{28,40},{32,4... | collective-permute-start | bytes 786440 | tf_op jit(solution)/shard_map/ppermute | solution.py:19
  147.9 56.3 %collective-permute-start.4 = (bf16[512,2,128]{2,0,1:T(8,128)(2,1)}, bf16[512,2,128]{2,0,1:T(8,128)(2,1)}, u32[]{:S(2)}, u32[]{:S(2)}) collective-permute-start(bf16[512,2,128]{2,0,1:T(8,128)(2,1)} %pad_maximum_fusion.2), channel_id=1, source_target_pairs={{0,16},{4,20},{8,24},{12,28},{16,32},{20,36},{24,40},{28,44},{32,4... | collective-permute-start | bytes 786440 | tf_op jit(solution)/shard_map/ppermute | solution.py:19
  150.2 6.5 %copy-start.3 = (bf16[512,4096]{1,0:T(8,128)(2,1)S(1)}, bf16[512,4096]{1,0:T(8,128)(2,1)}, u32[]{:S(2)}) copy-start(bf16[512,4096]{1,0:T(8,128)(2,1)} %copy-done.2) | copy-start | bytes 12582916
  172.6 91.5 %collective-permute-start.3 = (bf16[512,2,128]{0,2,1:T(8,128)(2,1)}, bf16[512,2,128]{0,2,1:T(8,128)(2,1)}, u32[]{:S(2)}, u32[]{:S(2)}) collective-permute-start(bf16[512,2,128]{0,2,1:T(8,128)(2,1)} %bitcast.126), channel_id=1, source_target_pairs={{0,4},{4,8},{8,12},{12,16},{16,20},{20,24},{24,28},{28,32},{32,36}... | collective-permute-start | bytes 786440 | tf_op jit(solution)/shard_map/ppermute | solution.py:19
  201.7 1.0 copy-start.9
  201.7 1.0 copy-start.11
  202.7 1.4 copy-start.13
  204.2 59.9 %collective-permute-start.2 = (bf16[512,2,128]{0,2,1:T(8,128)(2,1)S(1)}, bf16[512,2,128]{0,2,1:T(8,128)(2,1)S(1)}, u32[]{:S(2)}, u32[]{:S(2)}) collective-permute-start(bf16[512,2,128]{0,2,1:T(8,128)(2,1)S(1)} %bitcast.127), channel_id=1, source_target_pairs={{0,8},{4,12},{8,16},{12,20},{16,24},{20,28},{24,32},{28,36},{32,40... | collective-permute-start | bytes 786440 | tf_op jit(solution)/shard_map/ppermute | solution.py:19
  208.9 55.1 %collective-permute-start.1 = (bf16[512,2,128]{0,2,1:T(8,128)(2,1)S(1)}, bf16[512,2,128]{0,2,1:T(8,128)(2,1)S(1)}, u32[]{:S(2)}, u32[]{:S(2)}) collective-permute-start(bf16[512,2,128]{0,2,1:T(8,128)(2,1)S(1)} %bitcast.128), channel_id=1, source_target_pairs={{0,12},{4,16},{8,20},{12,24},{16,28},{20,32},{24,36},{28,40},{32,4... | collective-permute-start | bytes 786440 | tf_op jit(solution)/shard_map/ppermute | solution.py:19
  215.7 7.1 %copy-start.5 = (bf16[512,2,64]{2,0,1:T(8,128)(2,1)S(1)}, bf16[512,2,64]{2,0,1:T(8,128)(2,1)}, u32[]{:S(2)}) copy-start(bf16[512,2,64]{2,0,1:T(8,128)(2,1)} %copy-done.4) | copy-start | bytes 393220
  215.7 7.1 %copy-start.7 = (bf16[512,2,64]{2,0,1:T(8,128)(2,1)S(1)}, bf16[512,2,64]{2,0,1:T(8,128)(2,1)}, u32[]{:S(2)}) copy-start(bf16[512,2,64]{2,0,1:T(8,128)(2,1)} %copy-done.6) | copy-start | bytes 393220
  215.7 48.2 %collective-permute-start = (bf16[512,2,128]{0,2,1:T(8,128)(2,1)S(1)}, bf16[512,2,128]{0,2,1:T(8,128)(2,1)S(1)}, u32[]{:S(2)}, u32[]{:S(2)}) collective-permute-start(bf16[512,2,128]{0,2,1:T(8,128)(2,1)S(1)} %bitcast.129), channel_id=1, source_target_pairs={{0,16},{4,20},{8,24},{12,28},{16,32},{20,36},{24,40},{28,44},{32,4... | collective-permute-start | bytes 786440 | tf_op jit(solution)/shard_map/ppermute | solution.py:19
  265.1 6.5 %copy-start.14 = (bf16[2560,2,128]{0,2,1:T(8,128)(2,1)}, bf16[2560,2,128]{0,2,1:T(8,128)(2,1)S(1)}, u32[]{:S(2)}) copy-start(bf16[2560,2,128]{0,2,1:T(8,128)(2,1)S(1)} %constant_dynamic-update-slice_fusion) | copy-start | bytes 3932164
  271.6 10.2 %copy-start.12 = (bf16[512,4,128]{0,2,1:T(8,128)(2,1)S(1)}, bf16[512,4,128]{0,2,1:T(8,128)(2,1)}, u32[]{:S(2)}) copy-start(bf16[512,4,128]{0,2,1:T(8,128)(2,1)} %divide_convert_fusion.1) | copy-start | bytes 1572868
  271.6 11.6 %copy-start.1 = (bf16[4096,256]{1,0:T(8,128)(2,1)S(1)}, bf16[4096,256]{1,0:T(8,128)(2,1)}, u32[]{:S(2)}) copy-start(bf16[4096,256]{1,0:T(8,128)(2,1)} %param.15) | copy-start | bytes 6291460
Sparse Core Ops, SparseCore 0:
  16.1 109.2 all-reduce.2
  127.1 30.7 all-gather.2
  159.5 30.9 all-gather.4
where the time goes:
time: 291 us; the launch traced here: 290 us
  waiting for transfers between devices  121 us (42%)
  matrix products  73.8 us (25%)
  other arithmetic  36.3 us (12%)
  starting transfers between devices  29.2 us (10%)
  local copies, waits for them, and re-layouts  16.2 us (6%)
  between operations  13.6 us (5%)
    psum x1, waiting for transfers between devices, body(): lax.psum(selector(query_up_maps).astype(jnp.bfloat16), 'tok')  106 us
    ppermute x8, starting transfers between devices, from_behind(): return lax.ppermute(x, axis, pairs)  29.2 us
    dot_general x10, matrix products, dense_scores(): jnp.einsum('qgd,kd->gqk', q_group, block_keys, preferred_element_type=jnp...  24.5 us
    reduce_sum x2, other arithmetic, body(): totals = jnp.sum(weights, axis=-1)  20.2 us
    dot_general x2, matrix products, body(): jnp.einsum('gqk,kd->qgd', probs, all_values[:, kv_group, :], preferred_el...  16.6 us
    all_gather x1, waiting for transfers between devices, body(): lax.all_gather(query_down_table, 'mlp', axis=2, tiled=True)  14.5 us
    dot_general x1, matrix products, body(): jnp.dot(normed_input, query_weight, preferred_element_type=jnp.float32)  8.29 us
    dot_general x4, matrix products, selector(): jnp.einsum('th,hrc->trc', picker, stored, preferred_element_type=jnp.floa...  6.56 us
  transfers between devices with their start and end apart: 11, of which 2 were waited for; matrix products, arithmetic and copies ran while one was open for 33% of the time, Pallas kernels for 0%

commit v1 on v0

v1 whole, which is shorter than its diff:
```python
import functools

import jax
import jax.numpy as jnp
import numpy as np
from jax import lax
from jax.experimental import pallas as pl
from jax.experimental.pallas import tpu as pltpu
from jax.sharding import PartitionSpec as P

WIDTH = 4096
HEAD = 128
RANK = 16
TENANTS = 16
ROWS = 512
HELD = 8
QCOLS = 1024
KVCOLS = 256
BACK = 4
N_TOK = 32
SIDE = 4
NORM_EPS = 1e-05
ROPE_BASE = 500000.0
ADAPTER_SCALE = 0.5
MESH = pl.DeviceIdType.MESH
F32 = jnp.float32
BF16 = jnp.bfloat16
SLAB = TENANTS * RANK
V_ROWS = (1024 + KVCOLS) // 128 * SLAB
Q_ROWS = (1024 + QCOLS) // 128 * SLAB
NORM_STEP = 32
COPIES = 14


def prompt_bounds(len_ref):
    starts, ends = [], []
    at = jnp.int32(0)
    for t in range(TENANTS):
        starts.append(at)
        at = at + len_ref[t]
        ends.append(at)
    return starts, ends


class AllReduce:
    def __init__(self, place, rows, mine, from_core, from_a, from_b, full, send, recv):
        self.place, self.rows = place, rows
        self.mine, self.from_core, self.from_a, self.from_b = mine, from_core, from_a, from_b
        self.full, self.send, self.recv = full, send, recv
        p = place
        half, quarter, piece = rows // 2, rows // 8, rows // 32
        self.half_at = pl.multiple_of(p["core"] * half, 16)
        self.other_at = pl.multiple_of((1 - p["core"]) * half, 16)
        self.a_at = pl.multiple_of(p["core"] * half + p["ca"] * quarter, 16)
        self.b_at = pl.multiple_of(p["core"] * half + p["ca"] * quarter + p["cb"] * piece, 16)

    def copy(self, slot, src, dst, dev):
        return pltpu.make_async_remote_copy(
            src_ref=src, dst_ref=dst, send_sem=self.send.at[slot], recv_sem=self.recv.at[slot],
            device_id=dev, device_id_type=MESH,
        )

    def copies(self, stage):
        p = self.place
        half, quarter, piece = self.rows // 2, self.rows // 8, self.rows // 32
        if stage == 0:
            return [self.copy(0, self.mine.at[pl.ds(self.other_at, half)], self.from_core, p["sib"])]
        if stage == 5:
            ref = self.full.at[pl.ds(self.half_at, half)]
            return [self.copy(13, ref, ref, p["sib"])]
        out = []
        for k in range(1, SIDE):
            a, b = (p["ca"] + k) % SIDE, (p["cb"] + k) % SIDE
            if stage == 1:
                at = pl.multiple_of(p["core"] * half + a * quarter, 16)
                out.append(self.copy(k, self.mine.at[pl.ds(at, quarter)], self.from_a.at[k - 1], p["peer_a"][k]))
            if stage == 2:
                at = pl.multiple_of(p["core"] * half + p["ca"] * quarter + b * piece, 16)
                out.append(self.copy(3 + k, self.mine.at[pl.ds(at, piece)], self.from_b.at[k - 1], p["peer_b"][k]))
            if stage == 3:
                ref = self.full.at[pl.ds(self.b_at, piece)]
                out.append(self.copy(6 + k, ref, ref, p["peer_b"][k]))
            if stage == 4:
                ref = self.full.at[pl.ds(self.a_at, quarter)]
                out.append(self.copy(9 + k, ref, ref, p["peer_a"][k]))
        return out

    def start(self, stage):
        for c in self.copies(stage):
            c.start()

    def arrive(self, stage):
        for c in self.copies(stage):
            c.wait()
        half, quarter, piece = self.rows // 2, self.rows // 8, self.rows // 32
        if stage == 0:
            at = pl.ds(self.half_at, half)
            self.mine[at, :] = self.mine[at, :] + self.from_core[...]
        if stage == 1:
            at = pl.ds(self.a_at, quarter)
            self.mine[at, :] = (self.mine[at, :] + self.from_a[0]) + (self.from_a[1] + self.from_a[2])
        if stage == 2:
            at = pl.ds(self.b_at, piece)
            self.full[at, :] = (self.mine[at, :] + self.from_b[0]) + (self.from_b[1] + self.from_b[2])

    def step(self, stage):
        self.arrive(stage)
        self.start(stage + 1)


def project_kernel(
    len_ref, tid_ref, table_ref,
    x_hbm, gain_ref, wq_hbm, wk_hbm, wv_hbm, qd_hbm, vd_hbm, qu_hbm, vu_hbm,
    q_out, k_win, v_win,
    x, normed, w, base, qd, vd, qu, vu,
    mine_v, core_v, a_v, b_v, full_v,
    mine_q, core_q, a_q, b_q, full_q,
    cosine, sine, fold_v, got_v, fold_q, got_q, spread, k_own, v_own, q_own,
    ad_sem, x_sem, w_sem, sv, rv, sq, rq, z_send, z_recv, kv_send, kv_recv, own_sem,
):
    me = lax.axis_index("tok")
    z = lax.axis_index("mlp")
    core = lax.rem(me, 2)
    chip = me // 2
    px, py = lax.rem(chip, SIDE), chip // SIDE

    def tok_of(yy, xx, cc):
        return (yy * SIDE + xx) * 2 + cc

    sib = (me + 1 - 2 * core, z)
    ca = px * (1 - core) + py * core
    cb = py * (1 - core) + px * core
    peer_a, peer_b, peer_z = {}, {}, {}
    for k in range(1, SIDE):
        xk, yk = (px + k) % SIDE, (py + k) % SIDE
        along_x = tok_of(py, xk, core)
        along_y = tok_of(yk, px, core)
        peer_a[k] = (along_x * (1 - core) + along_y * core, z)
        peer_b[k] = (along_y * (1 - core) + along_x * core, z)
        peer_z[k] = (me, (z + k) % SIDE)
    ahead = ((me + 2) % N_TOK, z)
    behind = ((me + N_TOK - 2) % N_TOK, z)
    place = dict(core=core, ca=ca, cb=cb, sib=sib, peer_a=peer_a, peer_b=peer_b)

    barrier = pltpu.get_barrier_semaphore()
    greeted = [sib, ahead, behind] + [d[k] for d in (peer_a, peer_b, peer_z) for k in range(1, SIDE)]
    for dev in greeted:
        pl.semaphore_signal(barrier, inc=1, device_id=dev, device_id_type=MESH)

    loads = [
        pltpu.make_async_copy(src, dst, ad_sem.at[i])
        for i, (src, dst) in enumerate([(vd_hbm, vd), (vu_hbm, vu), (qd_hbm, qd), (qu_hbm, qu)])
    ]
    for c in loads:
        c.start()
    x_loads = [
        pltpu.make_async_copy(x_hbm.at[pl.ds(64 * i, 64)], x.at[pl.ds(64 * i, 64)], x_sem.at[i])
        for i in range(8)
    ]
    for c in x_loads:
        c.start()
    w_loads = [
        pltpu.make_async_copy(wk_hbm, w.at[0], w_sem.at[0]),
        pltpu.make_async_copy(wv_hbm, w.at[1], w_sem.at[1]),
    ] + [
        pltpu.make_async_copy(wq_hbm.at[:, pl.ds(256 * i, 256)], w.at[2 + i], w_sem.at[2 + i])
        for i in range(4)
    ]
    for c in w_loads:
        c.start()

    starts, ends = prompt_bounds(len_ref)
    for c in loads:
        c.wait()

    def gather(t, carry):
        local = table_ref[tid_ref[t]] - me * HELD
        held = jnp.logical_and(local >= 0, local < HELD)
        at = jnp.clip(local, 0, HELD - 1)

        def put(stored, target, first, slabs):
            for s in range(slabs):
                tile = stored[at, :, s * 128 : (s + 1) * 128]
                row = pl.multiple_of((first + s) * SLAB + t * RANK, RANK)
                target[pl.ds(row, RANK), :] = jnp.where(held, tile, jnp.zeros_like(tile))

        put(vd, mine_v, 0, 8)
        put(vu, mine_v, 8, 2)
        put(qd, mine_q, 0, 8)
        put(qu, mine_q, 8, 8)
        return carry

    lax.fori_loop(0, TENANTS, gather, 0)

    pl.semaphore_wait(barrier, len(greeted))
    red_v = AllReduce(place, V_ROWS, mine_v, core_v, a_v, b_v, full_v, sv, rv)
    red_q = AllReduce(place, Q_ROWS, mine_q, core_q, a_q, b_q, full_q, sq, rq)
    red_v.start(0)
    red_q.start(0)

    def angles(i, carry):
        row = pl.multiple_of(i * 64, 64)
        token = me * ROWS + row + lax.broadcasted_iota(jnp.int32, (64, HEAD), 0)
        begin = jnp.zeros((64, HEAD), jnp.int32)
        for t in range(TENANTS):
            begin = jnp.where(token >= starts[t], starts[t], begin)
        lane = lax.broadcasted_iota(jnp.int32, (64, HEAD), 1)
        pair = jnp.where(lane >= HEAD // 2, lane - HEAD // 2, lane)
        inverse = jnp.exp(-(pair.astype(F32) * (2.0 / HEAD)) * np.float32(np.log(np.float32(ROPE_BASE))))
        angle = (token - begin).astype(F32) * inverse
        cosine[pl.ds(row, 64), :] = jnp.cos(angle)
        s = jnp.sin(angle)
        sine[pl.ds(row, 64), :] = jnp.where(lane >= HEAD // 2, s, -s)
        return carry

    lax.fori_loop(0, 8, angles, 0)

    def normalise(first, count):
        def one(i, carry):
            at = pl.ds(pl.multiple_of(i * NORM_STEP, NORM_STEP), NORM_STEP)
            wide = x[at, :].astype(F32)
            scale = lax.rsqrt(jnp.mean(wide * wide, axis=1, keepdims=True) + NORM_EPS)
            normed[at, :] = (wide * scale * gain_ref[...]).astype(BF16)
            return carry

        lax.fori_loop(first, first + count, one, 0)

    for i in range(4):
        x_loads[i].wait()
    normalise(0, 8)
    red_v.step(0)
    for i in range(4, 8):
        x_loads[i].wait()
    normalise(8, 8)
    red_q.step(0)

    def rope(block):
        return block * cosine[...] + pltpu.roll(block, HEAD // 2, 1) * sine[...]

    def win_copy(win, which, slot):
        group = 4 * which
        send, recv = kv_send.at[group + slot], kv_recv.at[group + slot]
        if slot == 0:
            src, dst, dev = win.at[4], win.at[2], ahead
        elif slot == 1:
            src, dst, dev = win.at[2], win.at[0], ahead
        elif slot == 2:
            src, dst, dev = win.at[4 - 2 * core], win.at[3], sib
        else:
            src, dst, dev = win.at[2 - 2 * core], win.at[1], sib
        return pltpu.make_async_remote_copy(
            src_ref=src, dst_ref=dst, send_sem=send, recv_sem=recv, device_id=dev, device_id_type=MESH
        )

    def product(j):
        w_loads_j = pltpu.make_async_copy(wk_hbm, w.at[j], w_sem.at[j])
        w_loads_j.wait()
        base[j] = jnp.dot(normed[...], w[j], preferred_element_type=F32)

    def table(full, first, slabs):
        return jnp.concatenate([full[(first + s) * SLAB : (first + s + 1) * SLAB, :] for s in range(slabs)], axis=1)

    def members():
        token = me * ROWS + lax.broadcasted_iota(jnp.int32, (RANK, ROWS), 1)
        return [jnp.logical_and(token >= starts[t], token < ends[t]) for t in range(TENANTS)]

    def shrink(full, fold, got, which):
        some = normed[:, pl.ds(pl.multiple_of(z * 1024, 1024), 1024)]
        sums = lax.dot_general(table(full, 0, 8), some, (((1,), (1,)), ((), ())), preferred_element_type=F32)
        mask = members()
        total = jnp.zeros((RANK, ROWS), F32)
        for t in range(TENANTS):
            total = total + jnp.where(mask[t], sums[t * RANK : (t + 1) * RANK, :], 0.0)
        fold[...] = total
        for c in shrink_copies(fold, got, which):
            c.start()

    def shrink_copies(fold, got, which):
        return [
            pltpu.make_async_remote_copy(
                src_ref=fold, dst_ref=got.at[k - 1], send_sem=z_send.at[3 * which + k - 1],
                recv_sem=z_recv.at[3 * which + k - 1], device_id=peer_z[k], device_id_type=MESH,
            )
            for k in range(1, SIDE)
        ]

    def expand(fold, got, which):
        for c in shrink_copies(fold, got, which):
            c.wait()
        total = ((fold[...] + got[0]) + (got[1] + got[2])).astype(BF16).astype(F32)
        mask = members()
        for t in range(TENANTS):
            spread[t * RANK : (t + 1) * RANK, :] = jnp.where(mask[t], total, 0.0).astype(BF16)

    def work(j, carry):
        product(j)

        @pl.when(j == 0)
        def _():
            for h in range(2):
                cols = slice(h * HEAD, (h + 1) * HEAD)
                k_own[:, cols] = rope(base[0, :, cols]).astype(BF16)
            c = pltpu.make_async_copy(k_own, k_win.at[4], own_sem.at[0])
            c.start()
            c.wait()
            win_copy(k_win, 0, 0).start()
            red_v.step(1)

        @pl.when(j == 1)
        def _():
            red_v.step(2)
            red_q.step(1)

        @pl.when(j == 2)
        def _():
            red_v.step(3)
            red_q.step(2)

        @pl.when(j == 3)
        def _():
            red_v.step(4)
            red_q.step(3)
        return carry

    lax.fori_loop(0, 6, work, 0)

    red_v.arrive(5)
    shrink(full_v, fold_v, got_v, 0)
    red_q.step(4)
    win_copy(k_win, 0, 0).wait()
    win_copy(k_win, 0, 1).start()
    win_copy(k_win, 0, 2).start()
    expand(fold_v, got_v, 0)
    delta = lax.dot_general(spread[...], table(full_v, 8, 2), (((0,), (0,)), ((), ())), preferred_element_type=F32)
    v_own[...] = (base[1] + ADAPTER_SCALE * delta).astype(BF16)
    c = pltpu.make_async_copy(v_own, v_win.at[4], own_sem.at[1])
    c.start()
    c.wait()
    win_copy(v_win, 1, 0).start()

    red_q.arrive(5)
    shrink(full_q, fold_q, got_q, 1)
    win_copy(k_win, 0, 1).wait()
    win_copy(k_win, 0, 3).start()
    win_copy(v_win, 1, 0).wait()
    win_copy(v_win, 1, 1).start()
    win_copy(v_win, 1, 2).start()
    expand(fold_q, got_q, 1)

    def query(j, carry):
        up = jnp.concatenate(
            [full_q[pl.ds(pl.multiple_of((8 + 2 * j + s) * SLAB, SLAB), SLAB), :] for s in range(2)], axis=1
        )
        delta = lax.dot_general(spread[...], up, (((0,), (0,)), ((), ())), preferred_element_type=F32)
        rows = base[2 + j] + ADAPTER_SCALE * delta
        q_own[j] = jnp.concatenate([rope(rows[:, :HEAD]), rope(rows[:, HEAD:])], axis=1).astype(BF16)
        c = pltpu.make_async_copy(q_own.at[j], q_out.at[:, pl.ds(pl.multiple_of(j * 256, 256), 256)], own_sem.at[2 + j])
        c.start()
        return carry

    lax.fori_loop(0, 4, query, 0)
    for j in range(4):
        pltpu.make_async_copy(q_own.at[j], q_out.at[:, pl.ds(j * 256, 256)], own_sem.at[2 + j]).wait()
    win_copy(v_win, 1, 1).wait()
    win_copy(v_win, 1, 3).start()
    for s in (2, 3):
        win_copy(k_win, 0, s).wait()
    for s in (2, 3):
        win_copy(v_win, 1, s).wait()


def project(x, gain, wq, wk, wv, qd, vd, qu, vu, lengths, tid, slots):
    any_space = pl.BlockSpec(memory_space=pl.ANY)
    smem = pl.BlockSpec(memory_space=pltpu.SMEM)
    vmem = pl.BlockSpec(memory_space=pltpu.VMEM)
    dma = pltpu.SemaphoreType.DMA

    def reduce_scratch(rows):
        return [
            pltpu.VMEM((rows, 128), BF16),
            pltpu.VMEM((rows // 2, 128), BF16),
            pltpu.VMEM((3, rows // 8, 128), BF16),
            pltpu.VMEM((3, rows // 32, 128), BF16),
            pltpu.VMEM((rows, 128), BF16),
        ]

    return pl.pallas_call(
        project_kernel,
        out_shape=(
            jax.ShapeDtypeStruct((ROWS, QCOLS), BF16),
            jax.ShapeDtypeStruct((BACK + 1, ROWS, KVCOLS), BF16),
            jax.ShapeDtypeStruct((BACK + 1, ROWS, KVCOLS), BF16),
        ),
        in_specs=[smem] * 3 + [any_space, vmem] + [any_space] * 7,
        out_specs=(any_space, any_space, any_space),
        scratch_shapes=[
            pltpu.VMEM((ROWS, WIDTH), BF16),
            pltpu.VMEM((ROWS, WIDTH), BF16),
            pltpu.VMEM((6, WIDTH, 256), BF16),
            pltpu.VMEM((6, ROWS, 256), F32),
            pltpu.VMEM((HELD, RANK, 1024), BF16),
            pltpu.VMEM((HELD, RANK, 1024), BF16),
            pltpu.VMEM((HELD, RANK, QCOLS), BF16),
            pltpu.VMEM((HELD, RANK, KVCOLS), BF16),
        ]
        + reduce_scratch(V_ROWS)
        + reduce_scratch(Q_ROWS)
        + [
            pltpu.VMEM((ROWS, HEAD), F32),
            pltpu.VMEM((ROWS, HEAD), F32),
            pltpu.VMEM((RANK, ROWS), F32),
            pltpu.VMEM((3, RANK, ROWS), F32),
            pltpu.VMEM((RANK, ROWS), F32),
            pltpu.VMEM((3, RANK, ROWS), F32),
            pltpu.VMEM((SLAB, ROWS), BF16),
            pltpu.VMEM((ROWS, KVCOLS), BF16),
            pltpu.VMEM((ROWS, KVCOLS), BF16),
            pltpu.VMEM((4, ROWS, 256), BF16),
            dma((4,)), dma((8,)), dma((6,)),
            dma((COPIES,)), dma((COPIES,)), dma((COPIES,)), dma((COPIES,)),
            dma((6,)), dma((6,)), dma((8,)), dma((8,)), dma((6,)),
        ],
        compiler_params=pltpu.CompilerParams(
            collective_id=0, has_side_effects=True, vmem_limit_bytes=56 * 1024 * 1024
        ),
        name="project",
    )(lengths, tid, slots, x, gain, wq, wk, wv, qd, vd, qu, vu)


QT = 256
KC = 256


def attend_kernel(len_ref, q_ref, k_ref, v_ref, o_ref, m_ref, l_ref, acc_ref):
    me = lax.axis_index("tok")
    r = pl.program_id(1)
    first = me * ROWS + r * QT
    origin = (me - BACK) * ROWS
    starts, _ = prompt_bounds(len_ref)
    lowest = jnp.int32(0)
    token = first + lax.broadcasted_iota(jnp.int32, (QT, KC), 0)
    begin = jnp.zeros((QT, KC), jnp.int32)
    for t in range(TENANTS):
        lowest = jnp.where(first >= starts[t], starts[t], lowest)
        begin = jnp.where(token >= starts[t], starts[t], begin)
    end = BACK * ROWS + (r + 1) * QT
    need = end - (lowest - origin)
    chunks = (need + KC - 1) // KC
    q = jnp.concatenate([q_ref[:, h * HEAD : (h + 1) * HEAD] for h in range(4)], axis=0)
    m_ref[...] = jnp.full(m_ref.shape, -1e30, F32)
    l_ref[...] = jnp.zeros(l_ref.shape, F32)
    acc_ref[...] = jnp.zeros(acc_ref.shape, F32)
    scale = np.float32(HEAD ** -0.5 * np.log2(np.e))

    def one(i, carry):
        at = pl.multiple_of(end - (i + 1) * KC, KC)
        kk = k_ref[pl.ds(at, KC), :]
        vv = v_ref[pl.ds(at, KC), :]
        s = lax.dot_general(q, kk, (((1,), (1,)), ((), ())), preferred_element_type=F32) * scale
        kpos = origin + at + lax.broadcasted_iota(jnp.int32, (QT, KC), 1)
        seen = jnp.logical_and(kpos >= begin, kpos <= token)
        bias = jnp.where(seen, 0.0, -jnp.inf)
        s = (s.reshape(4, QT, KC) + bias[None]).reshape(4 * QT, KC)
        old = m_ref[...]
        new = jnp.maximum(old, jnp.max(s, axis=1, keepdims=True))
        p = jnp.exp2(s - new[:, :1])
        fade = jnp.exp2(old - new)
        m_ref[...] = new
        l_ref[...] = l_ref[...] * fade + jnp.sum(p, axis=1, keepdims=True)
        acc_ref[...] = acc_ref[...] * fade + jnp.dot(p.astype(BF16), vv, preferred_element_type=F32)
        return carry

    lax.fori_loop(0, chunks, one, 0)
    out = acc_ref[...] / l_ref[...]
    for h in range(4):
        o_ref[:, h * HEAD : (h + 1) * HEAD] = out[h * QT : (h + 1) * QT, :].astype(BF16)


def attend(lengths, q, k_win, v_win):
    span = (BACK + 1) * ROWS
    k2 = k_win.reshape(span, KVCOLS)
    v2 = v_win.reshape(span, KVCOLS)
    return pl.pallas_call(
        attend_kernel,
        out_shape=jax.ShapeDtypeStruct((ROWS, QCOLS), BF16),
        grid=(2, ROWS // QT),
        in_specs=[
            pl.BlockSpec(memory_space=pltpu.SMEM),
            pl.BlockSpec((QT, 512), lambda g, r: (r, g)),
            pl.BlockSpec((span, HEAD), lambda g, r: (0, g)),
            pl.BlockSpec((span, HEAD), lambda g, r: (0, g)),
        ],
        out_specs=pl.BlockSpec((QT, 512), lambda g, r: (r, g)),
        scratch_shapes=[pltpu.VMEM((4 * QT, HEAD), F32)] * 3,
        compiler_params=pltpu.CompilerParams(vmem_limit_bytes=48 * 1024 * 1024),
        name="attend",
    )(lengths, q, k2, v2)


def body(
    layer_input, input_norm_gain, query_weight, key_weight, value_weight,
    query_down_maps, value_down_maps, query_up_maps, value_up_maps,
    tenant_prompt_length, tenant_adapter_id, adapter_storage_slot,
):
    q, k_win, v_win = project(
        layer_input, input_norm_gain.reshape(1, WIDTH), query_weight, key_weight, value_weight,
        query_down_maps, value_down_maps, query_up_maps, value_up_maps,
        tenant_prompt_length, tenant_adapter_id, adapter_storage_slot,
    )
    return attend(tenant_prompt_length, q, k_win, v_win)


def solution(mesh):
    placed = (
        P("tok", None), P(), P(None, "mlp"), P(None, "mlp"), P(None, "mlp"),
        P("tok", None, "mlp"), P("tok", None, "mlp"), P("tok", None, "mlp"), P("tok", None, "mlp"),
        P(), P(), P(),
    )
    return jax.shard_map(
        body, mesh=mesh, in_specs=placed, out_specs=P("tok", "mlp"), check_vma=False
    )
```

time: 291 us -> 134 us (0.46)
  the two profiles are of different devices: /device:TPU:1 before, /device:TPU:69 now
where the time goes in v1:
time: 134 us
  Pallas kernels  130 us (97%)
  local copies, waits for them, and re-layouts  3.85 us (3%)
    pallas_call x1, Pallas kernels, attend(): pl.pallas_call(attend_kernel, out_shape=jax.ShapeDtypeStruct((ROWS, QCOLS...  66.8 us
    pallas_call x1, Pallas kernels, project(): pl.pallas_call(project_kernel, out_shape=(jax.ShapeDtypeStruct((ROWS, QCO...  63.4 us
    unnamed x8, local copies, waits for them, and re-layouts  3.85 us

profile of v1, /device:TPU:69, one launch (start us, length us, event | category | flops | bytes accessed | tf_op | source)
XLA Modules:
  0.0 134.1 jit_solution(53334362939776788)
XLA Ops:
  0.0 0.0 copy-start.3
  0.0 63.4 %project.1 = (bf16[512,1024]{1,0:T(8,128)(2,1)}, bf16[5,512,256]{2,1,0:T(8,128)(2,1)}, bf16[5,512,256]{2,1,0:T(8,128)(2,1)}) custom-call(s32[16]{0:T(128)} %len_ref.3, s32[16]{0:T(128)} %tid_ref.1, s32[256]{0:T(256)} %table_ref.1, bf16[512,4096]{1,0:T(8,128)(2,1)} %x_hbm.1, f32[1,4096]{1,0:T(1,128)} %bitcast.5, bf16[4096,1024]{1,0:T(8,128)(2,1)} %wq_hbm.1, ...), custom_call_target="tpu_custom_call" | custom-call | tf_op jit(solution)/shard_map/project/pallas_call | solution.py:387
  63.4 0.0 copy-done.3
  63.4 0.0 copy-start
  63.5 1.3 copy-done
  64.8 0.0 copy-start.1
  64.8 1.3 copy-done.1
  66.1 0.0 copy-start.2
  66.1 1.2 copy-done.2
  67.3 66.8 %attend.1 = bf16[512,1024]{1,0:T(8,128)(2,1)} custom-call(s32[16]{0:T(128)S(1)} %copy-done.3, bf16[512,1024]{1,0:T(8,128)(2,1)S(1)} %copy-done.2, bf16[2560,256]{1,0:T(8,128)(2,1)S(1)} %bitcast.3, bf16[2560,256]{1,0:T(8,128)(2,1)S(1)} %bitcast.4), custom_call_target="tpu_custom_call" | custom-call | tf_op jit(solution)/shard_map/attend/pallas_call | solution.py:483
Async XLA Ops:
  0.0 63.4 %copy-start.3 = (s32[16]{0:T(128)S(1)}, s32[16]{0:T(128)}, u32[]{:S(2)}) copy-start(s32[16]{0:T(128)} %len_ref.3) | copy-start | bytes 196
  63.4 1.3 copy-start
  64.8 1.3 copy-start.1
  66.1 1.2 copy-start.2

commit v2 on v1

--- a/solution.py
+++ b/solution.py
@@ -29,6 +29,11 @@
 V_ROWS = (1024 + KVCOLS) // 128 * SLAB
 Q_ROWS = (1024 + QCOLS) // 128 * SLAB
 NORM_STEP = 32
+SPAN = (BACK + 1) * ROWS
+FAR = 1e30
+QT = 256
+KC = 1152
+CHUNKS = (BACK * ROWS + QT) // KC
 COPIES = 14
 
 
@@ -108,15 +113,16 @@
         self.start(stage + 1)
 
 
-def project_kernel(
+def block_kernel(
     len_ref, tid_ref, table_ref,
     x_hbm, gain_ref, wq_hbm, wk_hbm, wv_hbm, qd_hbm, vd_hbm, qu_hbm, vu_hbm,
-    q_out, k_win, v_win,
+    out,
     x, normed, w, base, qd, vd, qu, vu,
     mine_v, core_v, a_v, b_v, full_v,
     mine_q, core_q, a_q, b_q, full_q,
-    cosine, sine, fold_v, got_v, fold_q, got_q, spread, k_own, v_own, q_own,
-    ad_sem, x_sem, w_sem, sv, rv, sq, rq, z_send, z_recv, kv_send, kv_recv, own_sem,
+    cosine, sine, fold_v, got_v, fold_q, got_q, spread, k_win, v_win, q_own,
+    q_mark, k_mark, marked, scores, highest, peak, sums, mixed,
+    ad_sem, x_sem, w_sem, sv, rv, sq, rq, z_send, z_recv, kv_send, kv_recv,
 ):
     me = lax.axis_index("tok")
     z = lax.axis_index("mlp")
@@ -198,6 +204,8 @@
     red_v.start(0)
     red_q.start(0)
 
+    marks(starts, ends, me, q_mark, k_mark)
+
     def angles(i, carry):
         row = pl.multiple_of(i * 64, 64)
         token = me * ROWS + row + lax.broadcasted_iota(jnp.int32, (64, HEAD), 0)
@@ -237,17 +245,20 @@
     def rope(block):
         return block * cosine[...] + pltpu.roll(block, HEAD // 2, 1) * sine[...]
 
+    def block(win, i):
+        return win.at[pl.ds(pl.multiple_of(i * ROWS, ROWS), ROWS)]
+
     def win_copy(win, which, slot):
         group = 4 * which
         send, recv = kv_send.at[group + slot], kv_recv.at[group + slot]
         if slot == 0:
-            src, dst, dev = win.at[4], win.at[2], ahead
+            src, dst, dev = block(win, 4), block(win, 2), ahead
         elif slot == 1:
-            src, dst, dev = win.at[2], win.at[0], ahead
+            src, dst, dev = block(win, 2), block(win, 0), ahead
         elif slot == 2:
-            src, dst, dev = win.at[4 - 2 * core], win.at[3], sib
+            src, dst, dev = block(win, 4 - 2 * core), block(win, 3), sib
         else:
-            src, dst, dev = win.at[2 - 2 * core], win.at[1], sib
+            src, dst, dev = block(win, 2 - 2 * core), block(win, 1), sib
         return pltpu.make_async_remote_copy(
             src_ref=src, dst_ref=dst, send_sem=send, recv_sem=recv, device_id=dev, device_id_type=MESH
         )
@@ -299,10 +310,7 @@
         def _():
             for h in range(2):
                 cols = slice(h * HEAD, (h + 1) * HEAD)
-                k_own[:, cols] = rope(base[0, :, cols]).astype(BF16)
-            c = pltpu.make_async_copy(k_own, k_win.at[4], own_sem.at[0])
-            c.start()
-            c.wait()
+                k_win[BACK * ROWS :, cols] = rope(base[0, :, cols]).astype(BF16)
             win_copy(k_win, 0, 0).start()
             red_v.step(1)
 
@@ -332,10 +340,7 @@
     win_copy(k_win, 0, 2).start()
     expand(fold_v, got_v, 0)
     delta = lax.dot_general(spread[...], table(full_v, 8, 2), (((0,), (0,)), ((), ())), preferred_element_type=F32)
-    v_own[...] = (base[1] + ADAPTER_SCALE * delta).astype(BF16)
-    c = pltpu.make_async_copy(v_own, v_win.at[4], own_sem.at[1])
-    c.start()
-    c.wait()
+    v_win[BACK * ROWS :, :] = (base[1] + ADAPTER_SCALE * delta).astype(BF16)
     win_copy(v_win, 1, 0).start()
 
     red_q.arrive(5)
@@ -354,22 +359,98 @@
         delta = lax.dot_general(spread[...], up, (((0,), (0,)), ((), ())), preferred_element_type=F32)
         rows = base[2 + j] + ADAPTER_SCALE * delta
         q_own[j] = jnp.concatenate([rope(rows[:, :HEAD]), rope(rows[:, HEAD:])], axis=1).astype(BF16)
-        c = pltpu.make_async_copy(q_own.at[j], q_out.at[:, pl.ds(pl.multiple_of(j * 256, 256), 256)], own_sem.at[2 + j])
-        c.start()
         return carry
 
     lax.fori_loop(0, 4, query, 0)
-    for j in range(4):
-        pltpu.make_async_copy(q_own.at[j], q_out.at[:, pl.ds(j * 256, 256)], own_sem.at[2 + j]).wait()
     win_copy(v_win, 1, 1).wait()
     win_copy(v_win, 1, 3).start()
     for s in (2, 3):
         win_copy(k_win, 0, s).wait()
     for s in (2, 3):
         win_copy(v_win, 1, s).wait()
-
-
-def project(x, gain, wq, wk, wv, qd, vd, qu, vu, lengths, tid, slots):
+    attention(me, starts, ends, q_own, k_win, v_win, out, q_mark, k_mark, marked, scores, highest, peak, sums, mixed)
+
+
+def marks(starts, ends, me, q_mark, k_mark):
+    lane = lax.broadcasted_iota(jnp.int32, (1, HEAD), 1)
+    begin = jnp.full((1, HEAD), 2**30, jnp.int32)
+    end = jnp.full((1, HEAD), 2**30, jnp.int32)
+    for t in range(TENANTS):
+        begin = jnp.where(lane == t, starts[t], begin)
+        end = jnp.where(lane == t, ends[t], end)
+    begin = jnp.where(lane == TENANTS, -(2**30), begin)
+    end = jnp.where(lane == TENANTS, 0, end)
+
+    def inside(first, row):
+        token = first + row + lax.broadcasted_iota(jnp.int32, (128, HEAD), 0)
+        return jnp.logical_and(token >= begin, token < end)
+
+    def keys(i, carry):
+        row = pl.multiple_of(i * 128, 128)
+        k_mark[pl.ds(row, 128), :] = jnp.where(inside((me - BACK) * ROWS, row), 1.0, 0.0).astype(BF16)
+        return carry
+
+    lax.fori_loop(0, SPAN // 128, keys, 0)
+
+    def queries(i, carry):
+        row = pl.multiple_of(i * 128, 128)
+        open_to = jnp.logical_or(inside(me * ROWS, row), lane > TENANTS)
+        q_mark[pl.ds(row, 128), :] = jnp.where(open_to, 0.0, -FAR).astype(BF16)
+        return carry
+
+    lax.fori_loop(0, ROWS // 128, queries, 0)
+
+
+def attention(me, starts, ends, q_ref, k_win, v_win, out, q_mark, k_mark, marked, scores, highest, peak, sums, mixed):
+    scale = np.float32(HEAD**-0.5 * np.log2(np.e))
+
+    def unit(u, carry):
+        group, part = u // 2, lax.rem(u, 2)
+        rows = pl.ds(pl.multiple_of(part * QT, QT), QT)
+        head_cols = pl.ds(pl.multiple_of(group * HEAD, HEAD), HEAD)
+        for h in range(4):
+            marked[h * QT : (h + 1) * QT, :HEAD] = q_ref[
+                2 * group + h // 2, rows, (h % 2) * HEAD : (h % 2 + 1) * HEAD
+            ]
+            marked[h * QT : (h + 1) * QT, HEAD:] = q_mark[rows, :]
+        for i in range(CHUNKS):
+            at = pl.multiple_of(part * QT + i * KC, 128)
+            keys = jnp.concatenate([k_win[pl.ds(at, KC), head_cols], k_mark[pl.ds(at, KC), :]], axis=1)
+            s = lax.dot_general(marked[...], keys, (((1,), (1,)), ((), ())), preferred_element_type=F32)
+            if i == CHUNKS - 1:
+                seen = lax.broadcasted_iota(jnp.int32, (QT, QT), 0) >= lax.broadcasted_iota(jnp.int32, (QT, QT), 1)
+                tail = s[:, KC - QT :]
+                tail = jnp.concatenate(
+                    [jnp.where(seen, tail[h * QT : (h + 1) * QT, :], -FAR) for h in range(4)], axis=0
+                )
+                s = jnp.concatenate([s[:, : KC - QT], tail], axis=1)
+            scores[i] = s
+            top = s[:, :128]
+            for c in range(1, KC // 128):
+                top = jnp.maximum(top, s[:, c * 128 : (c + 1) * 128])
+            highest[...] = top if i == 0 else jnp.maximum(highest[...], top)
+        peak[...] = jnp.broadcast_to(jnp.max(highest[...], axis=1, keepdims=True) * scale, peak.shape)
+        for i in range(CHUNKS):
+            at = pl.multiple_of(part * QT + i * KC, 128)
+            s = scores[i]
+            ps = [jnp.exp2(s[:, c * 128 : (c + 1) * 128] * scale - peak[...]) for c in range(KC // 128)]
+            total = ps[0]
+            for p in ps[1:]:
+                total = total + p
+            probs = jnp.concatenate([p.astype(BF16) for p in ps], axis=1)
+            mix = jnp.dot(probs, v_win[pl.ds(at, KC), head_cols], preferred_element_type=F32)
+            sums[...] = total if i == 0 else sums[...] + total
+            mixed[...] = mix if i == 0 else mixed[...] + mix
+        result = mixed[...] / jnp.sum(sums[...], axis=1, keepdims=True)
+        for h in range(4):
+            cols = pl.ds(pl.multiple_of(group * 512 + h * HEAD, HEAD), HEAD)
+            out[rows, cols] = result[h * QT : (h + 1) * QT, :].astype(BF16)
+        return carry
+
+    lax.fori_loop(0, 4, unit, 0)
+
+
+def block(x, gain, wq, wk, wv, qd, vd, qu, vu, lengths, tid, slots):
     any_space = pl.BlockSpec(memory_space=pl.ANY)
     smem = pl.BlockSpec(memory_space=pltpu.SMEM)
     vmem = pl.BlockSpec(memory_space=pltpu.VMEM)
@@ -385,14 +466,10 @@
         ]
 
     return pl.pallas_call(
-        project_kernel,
-        out_shape=(
-            jax.ShapeDtypeStruct((ROWS, QCOLS), BF16),
-            jax.ShapeDtypeStruct((BACK + 1, ROWS, KVCOLS), BF16),
-            jax.ShapeDtypeStruct((BACK + 1, ROWS, KVCOLS), BF16),
-        ),
+        block_kernel,
+        out_shape=jax.ShapeDtypeStruct((ROWS, QCOLS), BF16),
         in_specs=[smem] * 3 + [any_space, vmem] + [any_space] * 7,
-        out_specs=(any_space, any_space, any_space),
+        out_specs=vmem,
         scratch_shapes=[
             pltpu.VMEM((ROWS, WIDTH), BF16),
             pltpu.VMEM((ROWS, WIDTH), BF16),
@@ -413,88 +490,25 @@
             pltpu.VMEM((RANK, ROWS), F32),
             pltpu.VMEM((3, RANK, ROWS), F32),
             pltpu.VMEM((SLAB, ROWS), BF16),
-            pltpu.VMEM((ROWS, KVCOLS), BF16),
-            pltpu.VMEM((ROWS, KVCOLS), BF16),
+            pltpu.VMEM((SPAN, KVCOLS), BF16),
+            pltpu.VMEM((SPAN, KVCOLS), BF16),
             pltpu.VMEM((4, ROWS, 256), BF16),
+            pltpu.VMEM((ROWS, HEAD), BF16),
+            pltpu.VMEM((SPAN, HEAD), BF16),
+            pltpu.VMEM((4 * QT, 2 * HEAD), BF16),
+            pltpu.VMEM((CHUNKS, 4 * QT, KC), F32),
+        ]
+        + [pltpu.VMEM((4 * QT, HEAD), F32)] * 4
+        + [
             dma((4,)), dma((8,)), dma((6,)),
             dma((COPIES,)), dma((COPIES,)), dma((COPIES,)), dma((COPIES,)),
-            dma((6,)), dma((6,)), dma((8,)), dma((8,)), dma((6,)),
+            dma((6,)), dma((6,)), dma((8,)), dma((8,)),
         ],
         compiler_params=pltpu.CompilerParams(
-            collective_id=0, has_side_effects=True, vmem_limit_bytes=56 * 1024 * 1024
+            collective_id=0, has_side_effects=True, vmem_limit_bytes=60 * 1024 * 1024
         ),
-        name="project",
+        name="block",
     )(lengths, tid, slots, x, gain, wq, wk, wv, qd, vd, qu, vu)
-
-
-QT = 256
-KC = 256
-
-
-def attend_kernel(len_ref, q_ref, k_ref, v_ref, o_ref, m_ref, l_ref, acc_ref):
-    me = lax.axis_index("tok")
-    r = pl.program_id(1)
-    first = me * ROWS + r * QT
-    origin = (me - BACK) * ROWS
-    starts, _ = prompt_bounds(len_ref)
-    lowest = jnp.int32(0)
-    token = first + lax.broadcasted_iota(jnp.int32, (QT, KC), 0)
-    begin = jnp.zeros((QT, KC), jnp.int32)
-    for t in range(TENANTS):
-        lowest = jnp.where(first >= starts[t], starts[t], lowest)
-        begin = jnp.where(token >= starts[t], starts[t], begin)
-    end = BACK * ROWS + (r + 1) * QT
-    need = end - (lowest - origin)
-    chunks = (need + KC - 1) // KC
-    q = jnp.concatenate([q_ref[:, h * HEAD : (h + 1) * HEAD] for h in range(4)], axis=0)
-    m_ref[...] = jnp.full(m_ref.shape, -1e30, F32)
-    l_ref[...] = jnp.zeros(l_ref.shape, F32)
-    acc_ref[...] = jnp.zeros(acc_ref.shape, F32)
-    scale = np.float32(HEAD ** -0.5 * np.log2(np.e))
-
-    def one(i, carry):
-        at = pl.multiple_of(end - (i + 1) * KC, KC)
-        kk = k_ref[pl.ds(at, KC), :]
-        vv = v_ref[pl.ds(at, KC), :]
-        s = lax.dot_general(q, kk, (((1,), (1,)), ((), ())), preferred_element_type=F32) * scale
-        kpos = origin + at + lax.broadcasted_iota(jnp.int32, (QT, KC), 1)
-        seen = jnp.logical_and(kpos >= begin, kpos <= token)
-        bias = jnp.where(seen, 0.0, -jnp.inf)
-        s = (s.reshape(4, QT, KC) + bias[None]).reshape(4 * QT, KC)
-        old = m_ref[...]
-        new = jnp.maximum(old, jnp.max(s, axis=1, keepdims=True))
-        p = jnp.exp2(s - new[:, :1])
-        fade = jnp.exp2(old - new)
-        m_ref[...] = new
-        l_ref[...] = l_ref[...] * fade + jnp.sum(p, axis=1, keepdims=True)
-        acc_ref[...] = acc_ref[...] * fade + jnp.dot(p.astype(BF16), vv, preferred_element_type=F32)
-        return carry
-
-    lax.fori_loop(0, chunks, one, 0)
-    out = acc_ref[...] / l_ref[...]
-    for h in range(4):
-        o_ref[:, h * HEAD : (h + 1) * HEAD] = out[h * QT : (h + 1) * QT, :].astype(BF16)
-
-
-def attend(lengths, q, k_win, v_win):
-    span = (BACK + 1) * ROWS
-    k2 = k_win.reshape(span, KVCOLS)
-    v2 = v_win.reshape(span, KVCOLS)
-    return pl.pallas_call(
-        attend_kernel,
-        out_shape=jax.ShapeDtypeStruct((ROWS, QCOLS), BF16),
-        grid=(2, ROWS // QT),
-        in_specs=[
-            pl.BlockSpec(memory_space=pltpu.SMEM),
-            pl.BlockSpec((QT, 512), lambda g, r: (r, g)),
-            pl.BlockSpec((span, HEAD), lambda g, r: (0, g)),
-            pl.BlockSpec((span, HEAD), lambda g, r: (0, g)),
-        ],
-        out_specs=pl.BlockSpec((QT, 512), lambda g, r: (r, g)),
-        scratch_shapes=[pltpu.VMEM((4 * QT, HEAD), F32)] * 3,
-        compiler_params=pltpu.CompilerParams(vmem_limit_bytes=48 * 1024 * 1024),
-        name="attend",
-    )(lengths, q, k2, v2)
 
 
 def body(
@@ -502,12 +516,11 @@
     query_down_maps, value_down_maps, query_up_maps, value_up_maps,
     tenant_prompt_length, tenant_adapter_id, adapter_storage_slot,
 ):
-    q, k_win, v_win = project(
+    return block(
         layer_input, input_norm_gain.reshape(1, WIDTH), query_weight, key_weight, value_weight,
         query_down_maps, value_down_maps, query_up_maps, value_up_maps,
         tenant_prompt_length, tenant_adapter_id, adapter_storage_slot,
     )
-    return attend(tenant_prompt_length, q, k_win, v_win)
 
 
 def solution(mesh):

time: 134 us -> 83.1 us (0.62)
  the two profiles are of different devices: /device:TPU:69 before, /device:TPU:1 now
where the time goes in v2:
time: 83.1 us; the launch traced here: 82.9 us
  Pallas kernels  80.6 us (97%)
  local copies, waits for them, and re-layouts  2.26 us (3%)
    pallas_call x1, Pallas kernels, block(): pl.pallas_call(block_kernel, out_shape=jax.ShapeDtypeStruct((ROWS, QCOLS)...  80.6 us
    unnamed x1, local copies, waits for them, and re-layouts  2.26 us

profile of v2, /device:TPU:1, one launch (start us, length us, event | category | flops | bytes accessed | tf_op | source)
XLA Modules:
  0.0 82.9 jit_solution(4311954075560549332)
XLA Ops:
  0.0 80.6 %block.1 = bf16[512,1024]{1,0:T(8,128)(2,1)} custom-call(s32[16]{0:T(128)} %len_ref.1, s32[16]{0:T(128)} %tid_ref.1, s32[256]{0:T(256)} %table_ref.1, bf16[512,4096]{1,0:T(8,128)(2,1)} %x_hbm.1, f32[1,4096]{1,0:T(1,128)} %bitcast.1, bf16[4096,1024]{1,0:T(8,128)(2,1)} %wq_hbm.1, bf16[4096,256]{1,0:T(8,128)(2,1)} %wk_hbm.1, bf16[4096,256]{1,0:T(8,128)(2,1)} %wv_hbm.1, ...), custom_call_target="tpu_custom_call" | custom-call | tf_op jit(solution)/shard_map/block/pallas_call | solution.py:468
  80.6 2.3 %copy.14 = bf16[512,1024]{1,0:T(8,128)(2,1)} copy(bf16[512,1024]{1,0:T(8,128)(2,1)} %block.1) | data formatting | bytes 2097152

commit v3 on v2

v3 whole, which is shorter than its diff:
```python
import functools

import jax
import jax.numpy as jnp
import numpy as np
from jax import lax
from jax.experimental import pallas as pl
from jax.experimental.pallas import tpu as pltpu
from jax.sharding import PartitionSpec as P

WIDTH = 4096
HEAD = 128
RANK = 16
TENANTS = 16
ROWS = 512
HELD = 8
QCOLS = 1024
KVCOLS = 256
BACK = 4
N_TOK = 32
SIDE = 4
NORM_EPS = 1e-05
ROPE_BASE = 500000.0
ADAPTER_SCALE = 0.5
MESH = pl.DeviceIdType.MESH
F32 = jnp.float32
BF16 = jnp.bfloat16
SLAB = TENANTS * RANK
DOWN_ROWS = 2 * 1024 // 128 * SLAB
UP_ROWS = (QCOLS + KVCOLS) // 128 * SLAB
AHEAD = 3
NORM_STEP = 32
SPAN = (BACK + 1) * ROWS
FAR = 1e30
QT = 256
KC = 1152
CHUNKS = (BACK * ROWS + QT) // KC
UNITS = 4
SCALE = np.float32(HEAD**-0.5 * np.log2(np.e))
COPIES = 11
PARTS = 4


def prompt_bounds(len_ref):
    starts, ends = [], []
    at = jnp.int32(0)
    for t in range(TENANTS):
        starts.append(at)
        at = at + len_ref[t]
        ends.append(at)
    return starts, ends


class AllReduce:
    def __init__(self, place, rows, mine, from_core, from_a, from_b, full, send, recv):
        self.place, self.rows = place, rows
        self.mine, self.from_core, self.from_a, self.from_b = mine, from_core, from_a, from_b
        self.full, self.send, self.recv = full, send, recv
        p = place
        half, quarter = rows // 2, rows // 8
        self.half_at = pl.multiple_of(p["core"] * half, 16)
        self.other_at = pl.multiple_of((1 - p["core"]) * half, 16)
        self.a_at = pl.multiple_of(p["core"] * half + p["ca"] * quarter, 16)

    def copy(self, slot, src, dst, dev):
        return pltpu.make_async_remote_copy(
            src_ref=src, dst_ref=dst, send_sem=self.send.at[slot], recv_sem=self.recv.at[slot],
            device_id=dev, device_id_type=MESH,
        )

    def copies(self, stage):
        p = self.place
        half, quarter = self.rows // 2, self.rows // 8
        if stage == 0:
            return [self.copy(0, self.mine.at[pl.ds(self.other_at, half)], self.from_core, p["sib"])]
        if stage == 4:
            ref = self.full.at[pl.ds(self.half_at, half)]
            return [self.copy(10, ref, ref, p["sib"])]
        out = []
        for k in range(1, SIDE):
            if stage == 1:
                a = (p["ca"] + k) % SIDE
                at = pl.multiple_of(p["core"] * half + a * quarter, 16)
                out.append(self.copy(k, self.mine.at[pl.ds(at, quarter)], self.from_a.at[k - 1], p["peer_a"][k]))
            if stage == 2:
                ref = self.mine.at[pl.ds(self.a_at, quarter)]
                out.append(self.copy(3 + k, ref, self.from_b.at[k - 1], p["peer_b"][k]))
            if stage == 3:
                ref = self.full.at[pl.ds(self.a_at, quarter)]
                out.append(self.copy(6 + k, ref, ref, p["peer_a"][k]))
        return out

    def start(self, stage):
        for c in self.copies(stage):
            c.start()

    def arrive(self, stage):
        for c in self.copies(stage):
            c.wait()
        half, quarter = self.rows // 2, self.rows // 8
        if stage == 0:
            at = pl.ds(self.half_at, half)
            self.mine[at, :] = self.mine[at, :] + self.from_core[...]
        if stage == 1:
            at = pl.ds(self.a_at, quarter)
            self.mine[at, :] = (self.mine[at, :] + self.from_a[0]) + (self.from_a[1] + self.from_a[2])
        if stage == 2:
            at = pl.ds(self.a_at, quarter)
            self.full[at, :] = (self.mine[at, :] + self.from_b[0]) + (self.from_b[1] + self.from_b[2])

    def step(self, stage):
        self.arrive(stage)
        self.start(stage + 1)


def block_kernel(
    len_ref, tid_ref, table_ref,
    x_hbm, gain_ref, wq_hbm, wk_hbm, wv_hbm, qd_hbm, vd_hbm, qu_hbm, vu_hbm,
    out,
    base, quarter,
    mine_d, core_d, a_d, b_d, down,
    mine_u, core_u, a_u, b_u, up,
    cosine, sine, fold, got, shrunk_v, spread, k_win, v_win, passing, q_own,
    q_mark, k_mark, marked, highest, peak, sums, mixed,
    ad_sem, x_sem, w_sem, sd, rd, su, ru, z_send, z_recv, kv_send, kv_recv, pass_send, pass_recv, share_send, share_recv, s_send, s_recv,
):
    me = lax.axis_index("tok")
    z = lax.axis_index("mlp")
    core = lax.rem(me, 2)
    chip = me // 2
    px, py = lax.rem(chip, SIDE), chip // SIDE

    def tok_of(yy, xx, cc):
        return (yy * SIDE + xx) * 2 + cc

    sib = (me + 1 - 2 * core, z)
    x_first = 1 - core
    ca = px * x_first + py * (1 - x_first)
    cb = py * x_first + px * (1 - x_first)
    peer_a, peer_b, peer_z = {}, {}, {}
    for k in range(1, SIDE):
        xk, yk = (px + k) % SIDE, (py + k) % SIDE
        along_x = tok_of(py, xk, core)
        along_y = tok_of(yk, px, core)
        peer_a[k] = (along_x * x_first + along_y * (1 - x_first), z)
        peer_b[k] = (along_y * x_first + along_x * (1 - x_first), z)
        peer_z[k] = (me, (z + k) % SIDE)
    later = {k: ((me + k) % N_TOK, z) for k in range(1, BACK + 1)}
    earlier = {k: ((me + N_TOK - k) % N_TOK, z) for k in range(1, BACK + 1)}
    place = dict(core=core, ca=ca, cb=cb, sib=sib, peer_a=peer_a, peer_b=peer_b)

    barrier = pltpu.get_barrier_semaphore()
    over = (tok_of((py + px // 2) % SIDE, (px + 3) % SIDE, core), z)
    goal = (tok_of(py, (px + 3) % SIDE, core), z)
    under_x = (px + 1) % SIDE
    under = (tok_of((py + SIDE - under_x // 2) % SIDE, under_x, core), z)
    greeted = [sib, over, under] + [d[k] for d in (peer_a, peer_b, peer_z) for k in range(1, SIDE)]
    greeted += [d[k] for d in (later, earlier) for k in range(1, BACK + 1)]
    for dev in greeted:
        pl.semaphore_signal(barrier, inc=1, device_id=dev, device_id_type=MESH)

    starts, ends = prompt_bounds(len_ref)
    red_d = AllReduce(place, DOWN_ROWS, mine_d, core_d, a_d, b_d, down, sd, rd)
    red_u = AllReduce(place, UP_ROWS, mine_u, core_u, a_u, b_u, up, su, ru)

    def angles(i, carry):
        row = pl.multiple_of(i * 64, 64)
        token = me * ROWS + row + lax.broadcasted_iota(jnp.int32, (64, HEAD), 0)
        begin = jnp.zeros((64, HEAD), jnp.int32)
        for t in range(TENANTS):
            begin = jnp.where(token >= starts[t], starts[t], begin)
        lane = lax.broadcasted_iota(jnp.int32, (64, HEAD), 1)
        pair = jnp.where(lane >= HEAD // 2, lane - HEAD // 2, lane)
        inverse = jnp.exp(-(pair.astype(F32) * (2.0 / HEAD)) * np.float32(np.log(np.float32(ROPE_BASE))))
        angle = (token - begin).astype(F32) * inverse
        cosine[pl.ds(row, 64), :] = jnp.cos(angle)
        s = jnp.sin(angle)
        sine[pl.ds(row, 64), :] = jnp.where(lane >= HEAD // 2, s, -s)
        return carry


    def rope(block):
        return block * cosine[...] + pltpu.roll(block, HEAD // 2, 1) * sine[...]

    def rows_of(win, block, part, parts):
        size = ROWS // parts
        return win.at[pl.ds(pl.multiple_of(block * ROWS + part * size, size), size)]

    def win_copy(win, which, slot, part):
        at = (2 * which + slot) * PARTS + part
        if which == 0 or slot == 0:
            src, dst = rows_of(win, BACK - 2 * slot, part, PARTS), rows_of(win, 2 - 2 * slot, part, PARTS)
            dev = later[2]
        else:
            src, dst = rows_of(passing, 0, part, PARTS), rows_of(win, 0, part, PARTS)
            dev = goal
        return pltpu.make_async_remote_copy(
            src_ref=src, dst_ref=dst, send_sem=kv_send.at[at], recv_sem=kv_recv.at[at],
            device_id=dev, device_id_type=MESH,
        )

    def pass_copy(part):
        return pltpu.make_async_remote_copy(
            src_ref=rows_of(v_win, BACK, part, PARTS), dst_ref=rows_of(passing, 0, part, PARTS),
            send_sem=pass_send.at[part], recv_sem=pass_recv.at[part], device_id=over, device_id_type=MESH,
        )

    def share_copy(win, which, slot):
        src, dst = (4 - 2 * core, 3) if slot == 0 else (2 - 2 * core, 1)
        at = 2 * which + slot
        return pltpu.make_async_remote_copy(
            src_ref=rows_of(win, src, 0, 1), dst_ref=rows_of(win, dst, 0, 1),
            send_sem=share_send.at[at], recv_sem=share_recv.at[at], device_id=sib, device_id_type=MESH,
        )

    def table(full, first, slabs):
        return jnp.concatenate([full[(first + s) * SLAB : (first + s + 1) * SLAB, :] for s in range(slabs)], axis=1)

    def members(first):
        token = first + lax.broadcasted_iota(jnp.int32, (RANK, ROWS), 1)
        return [jnp.logical_and(token >= starts[t], token < ends[t]) for t in range(TENANTS)]

    def z_copies():
        return [
            pltpu.make_async_remote_copy(
                src_ref=fold, dst_ref=got.at[k - 1], send_sem=z_send.at[k - 1], recv_sem=z_recv.at[k - 1],
                device_id=peer_z[k], device_id_type=MESH,
            )
            for k in range(1, SIDE)
        ]

    def shrunk_copies():
        return [
            pltpu.make_async_remote_copy(
                src_ref=shrunk_v.at[BACK], dst_ref=shrunk_v.at[BACK - k], send_sem=s_send.at[k - 1],
                recv_sem=s_recv.at[k - 1], device_id=later[k], device_id_type=MESH,
            )
            for k in range(1, BACK + 1)
        ]

    def shrink():
        maps = jnp.concatenate([table(down, 0, 8), table(down, 8, 8)], axis=0)
        part = lax.dot_general(maps, quarter[...], (((1,), (1,)), ((), ())), preferred_element_type=F32)
        mask = members(me * ROWS)
        for i in range(2):
            total = jnp.zeros((RANK, ROWS), F32)
            for t in range(TENANTS):
                row = i * SLAB + t * RANK
                total = total + jnp.where(mask[t], part[row : row + RANK, :], 0.0)
            fold[i * RANK : (i + 1) * RANK, :] = total
        for c in z_copies():
            c.start()

    def shrunk():
        for c in z_copies():
            c.wait()
        total = ((fold[...] + got[0]) + (got[1] + got[2])).astype(BF16)
        shrunk_v[BACK] = total[RANK:, :]
        for c in shrunk_copies():
            c.start()
        spread_out(total[:RANK, :].astype(F32), me * ROWS)

    def step(reduction, stage):
        return lambda: reduction.step(stage)

    def spread_out(values, first):
        mask = members(first)
        for t in range(TENANTS):
            spread[t * RANK : (t + 1) * RANK, :] = jnp.where(mask[t], values, 0.0).astype(BF16)

    def keys():
        for h in range(2):
            cols = slice(h * HEAD, (h + 1) * HEAD)
            k_win[BACK * ROWS :, cols] = rope(base[0, :, cols]).astype(BF16)

    def values():
        v_win[BACK * ROWS :, :] = base[1].astype(BF16)

    def send(win, which, slot, *parts):
        def act():
            for part in parts:
                win_copy(win, which, slot, part).start()

        return act

    def send_k(*parts):
        return send(k_win, 0, 0, *parts)

    def send_v(*parts):
        return send(v_win, 1, 0, *parts)

    def forward_k(*parts):
        def act():
            for part in parts:
                win_copy(k_win, 0, 0, part).wait()
                win_copy(k_win, 0, 1, part).start()

        return act

    def pass_v(*parts):
        def act():
            for part in parts:
                pass_copy(part).start()

        return act

    def forward_v(*parts):
        def act():
            for part in parts:
                pass_copy(part).wait()
                win_copy(v_win, 1, 1, part).start()

        return act

    def share(win, which, slot):
        for part in range(PARTS):
            if which or slot:
                win_copy(win, which, slot, part).wait()
        share_copy(win, which, slot).start()

    def query(j, carry):
        cols = jnp.concatenate(
            [up[pl.ds(pl.multiple_of((2 * j + s) * SLAB, SLAB), SLAB), :] for s in range(2)], axis=1
        )
        delta = lax.dot_general(spread[...], cols, (((0,), (0,)), ((), ())), preferred_element_type=F32)
        rows = base[2 + j] + ADAPTER_SCALE * delta
        q_own[j] = jnp.concatenate([rope(rows[:, :HEAD]), rope(rows[:, HEAD:])], axis=1).astype(BF16)
        return carry

    def value(i, carry):
        at = pl.ds(pl.multiple_of(i * ROWS, ROWS), ROWS)
        spread_out(shrunk_v[i].astype(F32), (me - BACK + i) * ROWS)
        delta = lax.dot_general(
            spread[...], table(up, 8, 2), (((0,), (0,)), ((), ())), preferred_element_type=F32
        )
        own = jnp.where(i == BACK, base[1], v_win[at, :].astype(F32))
        v_win[at, :] = (own + ADAPTER_SCALE * delta).astype(BF16)
        return carry

    def wait_keys():
        for slot in range(2):
            share(k_win, 0, slot)
        for slot in range(2):
            share_copy(k_win, 0, slot).wait()

    def wait_values():
        for slot in range(2):
            share(v_win, 1, slot)
        for slot in range(2):
            share_copy(v_win, 1, slot).wait()
        for c in shrunk_copies():
            c.wait()
        lax.fori_loop(0, BACK + 1, value, 0)

    def last_part(scores):
        wait_keys()

        def ahead(u, carry):
            score(u, q_own, k_win, q_mark, k_mark, marked, scores, highest, peak)
            return carry

        lax.fori_loop(0, AHEAD, ahead, 0)
        wait_values()

        def behind(u, carry):
            mix(u, v_win, out, scores, peak, sums, mixed)

            @pl.when(u + AHEAD < UNITS)
            def _():
                score(u + AHEAD, q_own, k_win, q_mark, k_mark, marked, scores, highest, peak)

            return carry

        lax.fori_loop(0, UNITS, behind, 0)

    def first_part(x, normed, w, qd, vd, qu, vu):
        loads = [
            pltpu.make_async_copy(src, dst, ad_sem.at[i])
            for i, (src, dst) in enumerate([(qd_hbm, qd), (vd_hbm, vd), (qu_hbm, qu), (vu_hbm, vu)])
        ]
        for c in loads:
            c.start()
        x_loads = [
            pltpu.make_async_copy(x_hbm.at[pl.ds(64 * i, 64)], x.at[pl.ds(64 * i, 64)], x_sem.at[i])
            for i in range(8)
        ]
        for c in x_loads:
            c.start()
        w_loads = [
            pltpu.make_async_copy(wk_hbm, w.at[0], w_sem.at[0]),
            pltpu.make_async_copy(wv_hbm, w.at[1], w_sem.at[1]),
        ] + [
            pltpu.make_async_copy(wq_hbm.at[:, pl.ds(256 * i, 256)], w.at[2 + i], w_sem.at[2 + i])
            for i in range(4)
        ]
        for c in w_loads:
            c.start()


        def gather(target, pieces):
            def one(t, carry):
                local = table_ref[tid_ref[t]] - me * HELD
                held = jnp.logical_and(local >= 0, local < HELD)
                at = jnp.clip(local, 0, HELD - 1)
                for stored, first, slabs in pieces:
                    for s in range(slabs):
                        tile = stored[at, :, s * 128 : (s + 1) * 128]
                        row = pl.multiple_of((first + s) * SLAB + t * RANK, RANK)
                        target[pl.ds(row, RANK), :] = jnp.where(held, tile, jnp.zeros_like(tile))
                return carry

            lax.fori_loop(0, TENANTS, one, 0)


        for c in loads[:2]:
            c.wait()
        gather(mine_d, [(qd, 0, 8), (vd, 8, 8)])
        pl.semaphore_wait(barrier, len(greeted))
        red_d.start(0)
        for c in loads[2:]:
            c.wait()
        gather(mine_u, [(qu, 0, 8), (vu, 8, 2)])
        red_u.start(0)

        def normalise(first, count):
            def one(i, carry):
                at = pl.ds(pl.multiple_of(i * NORM_STEP, NORM_STEP), NORM_STEP)
                wide = x[at, :].astype(F32)
                scale = lax.rsqrt(jnp.mean(wide * wide, axis=1, keepdims=True) + NORM_EPS)
                normed[at, :] = (wide * scale * gain_ref[...]).astype(BF16)
                return carry

            lax.fori_loop(first, first + count, one, 0)


        red_d.step(0)
        for i in range(4):
            x_loads[i].wait()
        normalise(0, 8)
        for i in range(4, 8):
            x_loads[i].wait()
        normalise(8, 8)
        quarter[...] = normed[:, pl.ds(pl.multiple_of(z * 1024, 1024), 1024)]
        lax.fori_loop(0, 8, angles, 0)
        red_u.step(0)
        marks(starts, ends, me, q_mark, k_mark)

        def product(j):
            w_loads_j = pltpu.make_async_copy(wk_hbm, w.at[j], w_sem.at[j])
            w_loads_j.wait()
            base[j] = jnp.dot(normed[...], w[j], preferred_element_type=F32)


        plan = [
            [keys, step(red_d, 1), send_k(0, 1)],
            [values, send_k(2, 3), pass_v(0, 1)],
            [step(red_d, 2), step(red_u, 1), send_v(0, 1), pass_v(2, 3)],
            [forward_k(0, 1, 2, 3)],
            [step(red_d, 3), step(red_u, 2), forward_v(0, 1)],
            [send_v(2, 3)],
        ]

        def work(j, carry):
            product(j)
            for at, acts in enumerate(plan):

                @pl.when(j == at)
                def _(acts=acts):
                    for act in acts:
                        act()

            return carry

        lax.fori_loop(0, 6, work, 0)
        red_d.arrive(4)
        shrink()
        red_u.step(3)
        forward_v(2, 3)()
        shrunk()
        red_u.arrive(4)
        lax.fori_loop(0, 4, query, 0)

    pl.run_scoped(
        first_part,
        pltpu.VMEM((ROWS, WIDTH), BF16),
        pltpu.VMEM((ROWS, WIDTH), BF16),
        pltpu.VMEM((6, WIDTH, 256), BF16),
        pltpu.VMEM((HELD, RANK, 1024), BF16),
        pltpu.VMEM((HELD, RANK, 1024), BF16),
        pltpu.VMEM((HELD, RANK, QCOLS), BF16),
        pltpu.VMEM((HELD, RANK, KVCOLS), BF16),
    )
    pl.run_scoped(last_part, pltpu.VMEM((AHEAD, CHUNKS, 4 * QT, KC), F32))


def marks(starts, ends, me, q_mark, k_mark):
    lane = lax.broadcasted_iota(jnp.int32, (1, HEAD), 1)
    begin = jnp.full((1, HEAD), 2**30, jnp.int32)
    end = jnp.full((1, HEAD), 2**30, jnp.int32)
    for t in range(TENANTS):
        begin = jnp.where(lane == t, starts[t], begin)
        end = jnp.where(lane == t, ends[t], end)
    begin = jnp.where(lane == TENANTS, -(2**30), begin)
    end = jnp.where(lane == TENANTS, 0, end)

    def inside(first, row):
        token = first + row + lax.broadcasted_iota(jnp.int32, (128, HEAD), 0)
        return jnp.logical_and(token >= begin, token < end)

    def keys(i, carry):
        row = pl.multiple_of(i * 128, 128)
        k_mark[pl.ds(row, 128), :] = jnp.where(inside((me - BACK) * ROWS, row), 1.0, 0.0).astype(BF16)
        return carry

    lax.fori_loop(0, SPAN // 128, keys, 0)

    def queries(i, carry):
        row = pl.multiple_of(i * 128, 128)
        open_to = jnp.logical_or(inside(me * ROWS, row), lane > TENANTS)
        q_mark[pl.ds(row, 128), :] = jnp.where(open_to, 0.0, -FAR).astype(BF16)
        return carry

    lax.fori_loop(0, ROWS // 128, queries, 0)


def unit_of(u):
    group, part = u // 2, lax.rem(u, 2)
    rows = pl.ds(pl.multiple_of(part * QT, QT), QT)
    head_cols = pl.ds(pl.multiple_of(group * HEAD, HEAD), HEAD)
    return group, part, rows, head_cols


def score(u, q_ref, k_win, q_mark, k_mark, marked, scores, highest, peak):
    group, part, rows, head_cols = unit_of(u)
    slot = lax.rem(u, AHEAD)
    for h in range(4):
        marked[h * QT : (h + 1) * QT, :HEAD] = q_ref[
            2 * group + h // 2, rows, (h % 2) * HEAD : (h % 2 + 1) * HEAD
        ]
        marked[h * QT : (h + 1) * QT, HEAD:] = q_mark[rows, :]
    for i in range(CHUNKS):
        at = pl.multiple_of(part * QT + i * KC, 128)
        keys = jnp.concatenate([k_win[pl.ds(at, KC), head_cols], k_mark[pl.ds(at, KC), :]], axis=1)
        s = lax.dot_general(marked[...], keys, (((1,), (1,)), ((), ())), preferred_element_type=F32)
        if i == CHUNKS - 1:
            seen = lax.broadcasted_iota(jnp.int32, (QT, QT), 0) >= lax.broadcasted_iota(jnp.int32, (QT, QT), 1)
            tail = s[:, KC - QT :]
            tail = jnp.concatenate(
                [jnp.where(seen, tail[h * QT : (h + 1) * QT, :], -FAR) for h in range(4)], axis=0
            )
            s = jnp.concatenate([s[:, : KC - QT], tail], axis=1)
        scores[slot, i] = s
        top = s[:, :128]
        for c in range(1, KC // 128):
            top = jnp.maximum(top, s[:, c * 128 : (c + 1) * 128])
        highest[...] = top if i == 0 else jnp.maximum(highest[...], top)
    peak[slot] = jnp.broadcast_to(jnp.max(highest[...], axis=1, keepdims=True) * SCALE, highest.shape)


def mix(u, v_win, out, scores, peak, sums, mixed):
    group, part, rows, head_cols = unit_of(u)
    slot = lax.rem(u, AHEAD)
    for i in range(CHUNKS):
        at = pl.multiple_of(part * QT + i * KC, 128)
        s = scores[slot, i]
        top = peak[slot]
        ps = [jnp.exp2(s[:, c * 128 : (c + 1) * 128] * SCALE - top) for c in range(KC // 128)]
        total = ps[0]
        for p in ps[1:]:
            total = total + p
        probs = jnp.concatenate([p.astype(BF16) for p in ps], axis=1)
        product = jnp.dot(probs, v_win[pl.ds(at, KC), head_cols], preferred_element_type=F32)
        sums[...] = total if i == 0 else sums[...] + total
        mixed[...] = product if i == 0 else mixed[...] + product
    result = mixed[...] / jnp.sum(sums[...], axis=1, keepdims=True)
    for h in range(4):
        cols = pl.ds(pl.multiple_of(group * 512 + h * HEAD, HEAD), HEAD)
        out[rows, cols] = result[h * QT : (h + 1) * QT, :].astype(BF16)


def block(x, gain, wq, wk, wv, qd, vd, qu, vu, lengths, tid, slots):
    any_space = pl.BlockSpec(memory_space=pl.ANY)
    smem = pl.BlockSpec(memory_space=pltpu.SMEM)
    vmem = pl.BlockSpec(memory_space=pltpu.VMEM)
    dma = pltpu.SemaphoreType.DMA

    def reduce_scratch(rows):
        return [
            pltpu.VMEM((rows, 128), BF16),
            pltpu.VMEM((rows // 2, 128), BF16),
            pltpu.VMEM((3, rows // 8, 128), BF16),
            pltpu.VMEM((3, rows // 8, 128), BF16),
            pltpu.VMEM((rows, 128), BF16),
        ]

    return pl.pallas_call(
        block_kernel,
        out_shape=jax.ShapeDtypeStruct((ROWS, QCOLS), BF16),
        in_specs=[smem] * 3 + [any_space, vmem] + [any_space] * 7,
        out_specs=vmem,
        scratch_shapes=[
            pltpu.VMEM((6, ROWS, 256), F32),
            pltpu.VMEM((ROWS, 1024), BF16),
        ]
        + reduce_scratch(DOWN_ROWS)
        + reduce_scratch(UP_ROWS)
        + [
            pltpu.VMEM((ROWS, HEAD), F32),
            pltpu.VMEM((ROWS, HEAD), F32),
            pltpu.VMEM((2 * RANK, ROWS), F32),
            pltpu.VMEM((3, 2 * RANK, ROWS), F32),
            pltpu.VMEM((BACK + 1, RANK, ROWS), BF16),
            pltpu.VMEM((SLAB, ROWS), BF16),
            pltpu.VMEM((SPAN, KVCOLS), BF16),
            pltpu.VMEM((SPAN, KVCOLS), BF16),
            pltpu.VMEM((ROWS, KVCOLS), BF16),
            pltpu.VMEM((4, ROWS, 256), BF16),
            pltpu.VMEM((ROWS, HEAD), BF16),
            pltpu.VMEM((SPAN, HEAD), BF16),
            pltpu.VMEM((4 * QT, 2 * HEAD), BF16),
            pltpu.VMEM((4 * QT, HEAD), F32),
            pltpu.VMEM((AHEAD, 4 * QT, HEAD), F32),
        ]
        + [pltpu.VMEM((4 * QT, HEAD), F32)] * 2
        + [
            dma((4,)), dma((8,)), dma((6,)),
            *[dma((COPIES,))] * 4,
            dma((3,)), dma((3,)), dma((4 * PARTS,)), dma((4 * PARTS,)), dma((PARTS,)), dma((PARTS,)),
            dma((4,)), dma((4,)), dma((4,)), dma((4,)),
        ],
        compiler_params=pltpu.CompilerParams(
            collective_id=0, has_side_effects=True, vmem_limit_bytes=60 * 1024 * 1024
        ),
        name="block",
    )(lengths, tid, slots, x, gain, wq, wk, wv, qd, vd, qu, vu)


def body(
    layer_input, input_norm_gain, query_weight, key_weight, value_weight,
    query_down_maps, value_down_maps, query_up_maps, value_up_maps,
    tenant_prompt_length, tenant_adapter_id, adapter_storage_slot,
):
    return block(
        layer_input, input_norm_gain.reshape(1, WIDTH), query_weight, key_weight, value_weight,
        query_down_maps, value_down_maps, query_up_maps, value_up_maps,
        tenant_prompt_length, tenant_adapter_id, adapter_storage_slot,
    )


def solution(mesh):
    placed = (
        P("tok", None), P(), P(None, "mlp"), P(None, "mlp"), P(None, "mlp"),
        P("tok", None, "mlp"), P("tok", None, "mlp"), P("tok", None, "mlp"), P("tok", None, "mlp"),
        P(), P(), P(),
    )
    return jax.shard_map(
        body, mesh=mesh, in_specs=placed, out_specs=P("tok", "mlp"), check_vma=False
    )
```

time: 83.1 us -> 74 us (0.89)
  the two profiles are of different devices: /device:TPU:1 before, /device:TPU:17 now
where the time goes in v3:
time: 74 us; the launch traced here: 73.8 us
  Pallas kernels  71.5 us (97%)
  local copies, waits for them, and re-layouts  2.26 us (3%)
    pallas_call x1, Pallas kernels, block(): pl.pallas_call(block_kernel, out_shape=jax.ShapeDtypeStruct((ROWS, QCOLS)...  71.5 us
    unnamed x1, local copies, waits for them, and re-layouts  2.26 us

profile of v3, /device:TPU:17, one launch (start us, length us, event | category | flops | bytes accessed | tf_op | source)
XLA Modules:
  0.0 73.8 jit_solution(666474779980627752)
XLA Ops:
  0.0 71.5 %block.1 = bf16[512,1024]{1,0:T(8,128)(2,1)} custom-call(s32[16]{0:T(128)} %len_ref.1, s32[16]{0:T(128)} %tid_ref.1, s32[256]{0:T(256)} %table_ref.1, bf16[512,4096]{1,0:T(8,128)(2,1)} %x_hbm.1, f32[1,4096]{1,0:T(1,128)} %bitcast.1, bf16[4096,1024]{1,0:T(8,128)(2,1)} %wq_hbm.1, bf16[4096,256]{1,0:T(8,128)(2,1)} %wk_hbm.1, bf16[4096,256]{1,0:T(8,128)(2,1)} %wv_hbm.1, ...), custom_call_target="tpu_custom_call" | custom-call | tf_op jit(solution)/shard_map/block/pallas_call | solution.py:596
  71.5 2.3 %copy.14 = bf16[512,1024]{1,0:T(8,128)(2,1)} copy(bf16[512,1024]{1,0:T(8,128)(2,1)} %block.1) | data formatting | bytes 2097152

commit v4 on v3

--- a/solution.py
+++ b/solution.py
@@ -120,9 +120,9 @@
     base, quarter,
     mine_d, core_d, a_d, b_d, down,
     mine_u, core_u, a_u, b_u, up,
-    cosine, sine, fold, got, shrunk_v, spread, k_win, v_win, passing, q_own,
+    cosine, sine, fold, got, shrunk_v, spread, k_win, v_win, passing, turning, q_own,
     q_mark, k_mark, marked, highest, peak, sums, mixed,
-    ad_sem, x_sem, w_sem, sd, rd, su, ru, z_send, z_recv, kv_send, kv_recv, pass_send, pass_recv, share_send, share_recv, s_send, s_recv,
+    ad_sem, x_sem, w_sem, sd, rd, su, ru, z_send, z_recv, kv_send, kv_recv, pass_send, pass_recv, turn_send, turn_recv, turned, share_send, share_recv, s_send, s_recv,
 ):
     me = lax.axis_index("tok")
     z = lax.axis_index("mlp")
@@ -205,6 +205,23 @@
             send_sem=pass_send.at[part], recv_sem=pass_recv.at[part], device_id=over, device_id_type=MESH,
         )
 
+    at_turn = px == SIDE - 1
+    below = (tok_of((py + 1) % SIDE, px, core), z)
+    row_start = (tok_of(py, 0, core), z)
+
+    def turn_copy(part):
+        return pltpu.make_async_remote_copy(
+            src_ref=rows_of(v_win, BACK, part, PARTS), dst_ref=rows_of(turning, 0, part, PARTS),
+            send_sem=turn_send.at[part], recv_sem=turn_recv.at[part], device_id=below, device_id_type=MESH,
+        )
+
+    def turned_copy(part):
+        return pltpu.make_async_remote_copy(
+            src_ref=rows_of(turning, 0, part, PARTS), dst_ref=rows_of(v_win, 2, part, PARTS),
+            send_sem=turned.at[part], recv_sem=kv_recv.at[2 * PARTS + part], device_id=row_start,
+            device_id_type=MESH,
+        )
+
     def share_copy(win, which, slot):
         src, dst = (4 - 2 * core, 3) if slot == 0 else (2 - 2 * core, 1)
         at = 2 * which + slot
@@ -287,7 +304,31 @@
         return send(k_win, 0, 0, *parts)
 
     def send_v(*parts):
-        return send(v_win, 1, 0, *parts)
+        def act():
+            @pl.when(jnp.logical_not(at_turn))
+            def _():
+                send(v_win, 1, 0, *parts)()
+
+        return act
+
+    def turn_v(*parts):
+        def act():
+            @pl.when(at_turn)
+            def _():
+                for part in parts:
+                    turn_copy(part).start()
+
+        return act
+
+    def after_turn(*parts):
+        def act():
+            @pl.when(at_turn)
+            def _():
+                for part in parts:
+                    turn_copy(part).wait()
+                    turned_copy(part).start()
+
+        return act
 
     def forward_k(*parts):
         def act():
@@ -314,7 +355,18 @@
 
     def share(win, which, slot):
         for part in range(PARTS):
-            if which or slot:
+            if which == 1 and slot == 0:
+                win_copy(win, which, slot, part).wait_recv()
+
+                @pl.when(at_turn)
+                def _(part=part):
+                    turned_copy(part).wait_send()
+
+                @pl.when(jnp.logical_not(at_turn))
+                def _(part=part):
+                    win_copy(win, which, slot, part).wait_send()
+
+            elif which or slot:
                 win_copy(win, which, slot, part).wait()
         share_copy(win, which, slot).start()
 
@@ -453,11 +505,11 @@
 
         plan = [
             [keys, step(red_d, 1), send_k(0, 1)],
-            [values, send_k(2, 3), pass_v(0, 1)],
-            [step(red_d, 2), step(red_u, 1), send_v(0, 1), pass_v(2, 3)],
-            [forward_k(0, 1, 2, 3)],
-            [step(red_d, 3), step(red_u, 2), forward_v(0, 1)],
-            [send_v(2, 3)],
+            [values, turn_v(0, 1), send_k(2, 3)],
+            [step(red_d, 2), step(red_u, 1), pass_v(0, 1), turn_v(2, 3)],
+            [pass_v(2, 3)],
+            [step(red_d, 3), step(red_u, 2), forward_k(0, 1, 2, 3), after_turn(0, 1)],
+            [forward_v(0, 1), send_v(0, 1, 2, 3), after_turn(2, 3)],
         ]
 
         def work(j, carry):
@@ -614,6 +666,7 @@
             pltpu.VMEM((SPAN, KVCOLS), BF16),
             pltpu.VMEM((SPAN, KVCOLS), BF16),
             pltpu.VMEM((ROWS, KVCOLS), BF16),
+            pltpu.VMEM((ROWS, KVCOLS), BF16),
             pltpu.VMEM((4, ROWS, 256), BF16),
             pltpu.VMEM((ROWS, HEAD), BF16),
             pltpu.VMEM((SPAN, HEAD), BF16),
@@ -625,7 +678,7 @@
         + [
             dma((4,)), dma((8,)), dma((6,)),
             *[dma((COPIES,))] * 4,
-            dma((3,)), dma((3,)), dma((4 * PARTS,)), dma((4 * PARTS,)), dma((PARTS,)), dma((PARTS,)),
+            dma((3,)), dma((3,)), dma((4 * PARTS,)), dma((4 * PARTS,)), *[dma((PARTS,))] * 5,
             dma((4,)), dma((4,)), dma((4,)), dma((4,)),
         ],
         compiler_params=pltpu.CompilerParams(

time: 74 us -> 69.2 us (0.935)
  the two profiles are of different devices: /device:TPU:17 before, /device:TPU:1 now
where the time goes in v4:
time: 69.2 us; the launch traced here: 69 us
  Pallas kernels  66.7 us (96%)
  local copies, waits for them, and re-layouts  2.26 us (3%)
    pallas_call x1, Pallas kernels, block(): pl.pallas_call(block_kernel, out_shape=jax.ShapeDtypeStruct((ROWS, QCOLS)...  66.7 us
    unnamed x1, local copies, waits for them, and re-layouts  2.26 us

profile of v4, /device:TPU:1, one launch (start us, length us, event | category | flops | bytes accessed | tf_op | source)
XLA Modules:
  0.0 69.0 jit_solution(4321477954987221808)
XLA Ops:
  0.0 66.7 %block.1 = bf16[512,1024]{1,0:T(8,128)(2,1)} custom-call(s32[16]{0:T(128)} %len_ref.1, s32[16]{0:T(128)} %tid_ref.1, s32[256]{0:T(256)} %table_ref.1, bf16[512,4096]{1,0:T(8,128)(2,1)} %x_hbm.1, f32[1,4096]{1,0:T(1,128)} %bitcast.1, bf16[4096,1024]{1,0:T(8,128)(2,1)} %wq_hbm.1, bf16[4096,256]{1,0:T(8,128)(2,1)} %wk_hbm.1, bf16[4096,256]{1,0:T(8,128)(2,1)} %wv_hbm.1, ...), custom_call_target="tpu_custom_call" | custom-call | tf_op jit(solution)/shard_map/block/pallas_call | solution.py:648
  66.7 2.3 %copy.14 = bf16[512,1024]{1,0:T(8,128)(2,1)} copy(bf16[512,1024]{1,0:T(8,128)(2,1)} %block.1) | data formatting | bytes 2097152

commit v5 on v4

--- a/solution.py
+++ b/solution.py
@@ -115,14 +115,14 @@
 
 def block_kernel(
     len_ref, tid_ref, table_ref,
-    x_hbm, gain_ref, wq_hbm, wk_hbm, wv_hbm, qd_hbm, vd_hbm, qu_hbm, vu_hbm,
-    out,
-    base, quarter,
+    x_hbm, gain_hbm, wq_hbm, wk_hbm, wv_hbm, qd_hbm, vd_hbm, qu_hbm, vu_hbm,
+    out_hbm,
+    out, gain_ref, base, quarter,
     mine_d, core_d, a_d, b_d, down,
     mine_u, core_u, a_u, b_u, up,
     cosine, sine, fold, got, shrunk_v, spread, k_win, v_win, passing, turning, q_own,
     q_mark, k_mark, marked, highest, peak, sums, mixed,
-    ad_sem, x_sem, w_sem, sd, rd, su, ru, z_send, z_recv, kv_send, kv_recv, pass_send, pass_recv, turn_send, turn_recv, turned, share_send, share_recv, s_send, s_recv,
+    ad_sem, x_sem, w_sem, sd, rd, su, ru, gain_sem, out_sem, z_send, z_recv, kv_send, kv_recv, pass_send, pass_recv, turn_send, turn_recv, turned, share_send, share_recv, s_send, s_recv,
 ):
     me = lax.axis_index("tok")
     z = lax.axis_index("mlp")
@@ -404,6 +404,11 @@
             c.wait()
         lax.fori_loop(0, BACK + 1, value, 0)
 
+    def write(u):
+        group, part = u // 2, u % 2
+        at = (pl.ds(pl.multiple_of(part * QT, QT), QT), pl.ds(pl.multiple_of(group * 512, 512), 512))
+        return pltpu.make_async_copy(out.at[at], out_hbm.at[at], out_sem.at[u])
+
     def last_part(scores):
         wait_keys()
 
@@ -416,6 +421,7 @@
 
         def behind(u, carry):
             mix(u, v_win, out, scores, peak, sums, mixed)
+            write(u).start()
 
             @pl.when(u + AHEAD < UNITS)
             def _():
@@ -424,6 +430,8 @@
             return carry
 
         lax.fori_loop(0, UNITS, behind, 0)
+        for u in range(UNITS):
+            write(u).wait()
 
     def first_part(x, normed, w, qd, vd, qu, vu):
         loads = [
@@ -436,6 +444,8 @@
             pltpu.make_async_copy(x_hbm.at[pl.ds(64 * i, 64)], x.at[pl.ds(64 * i, 64)], x_sem.at[i])
             for i in range(8)
         ]
+        gain_load = pltpu.make_async_copy(gain_hbm, gain_ref, gain_sem.at[0])
+        gain_load.start()
         for c in x_loads:
             c.start()
         w_loads = [
@@ -467,6 +477,8 @@
         for c in loads[:2]:
             c.wait()
         gather(mine_d, [(qd, 0, 8), (vd, 8, 8)])
+        lax.fori_loop(0, 8, angles, 0)
+        marks(starts, ends, me, q_mark, k_mark)
         pl.semaphore_wait(barrier, len(greeted))
         red_d.start(0)
         for c in loads[2:]:
@@ -486,6 +498,7 @@
 
 
         red_d.step(0)
+        gain_load.wait()
         for i in range(4):
             x_loads[i].wait()
         normalise(0, 8)
@@ -493,9 +506,7 @@
             x_loads[i].wait()
         normalise(8, 8)
         quarter[...] = normed[:, pl.ds(pl.multiple_of(z * 1024, 1024), 1024)]
-        lax.fori_loop(0, 8, angles, 0)
         red_u.step(0)
-        marks(starts, ends, me, q_mark, k_mark)
 
         def product(j):
             w_loads_j = pltpu.make_async_copy(wk_hbm, w.at[j], w_sem.at[j])
@@ -593,7 +604,7 @@
     for i in range(CHUNKS):
         at = pl.multiple_of(part * QT + i * KC, 128)
         keys = jnp.concatenate([k_win[pl.ds(at, KC), head_cols], k_mark[pl.ds(at, KC), :]], axis=1)
-        s = lax.dot_general(marked[...], keys, (((1,), (1,)), ((), ())), preferred_element_type=F32)
+        s = lax.dot_general(marked[...], keys, (((1,), (1,)), ((), ())), preferred_element_type=F32) * SCALE
         if i == CHUNKS - 1:
             seen = lax.broadcasted_iota(jnp.int32, (QT, QT), 0) >= lax.broadcasted_iota(jnp.int32, (QT, QT), 1)
             tail = s[:, KC - QT :]
@@ -606,7 +617,7 @@
         for c in range(1, KC // 128):
             top = jnp.maximum(top, s[:, c * 128 : (c + 1) * 128])
         highest[...] = top if i == 0 else jnp.maximum(highest[...], top)
-    peak[slot] = jnp.broadcast_to(jnp.max(highest[...], axis=1, keepdims=True) * SCALE, highest.shape)
+    peak[slot] = jnp.broadcast_to(jnp.max(highest[...], axis=1, keepdims=True), highest.shape)
 
 
 def mix(u, v_win, out, scores, peak, sums, mixed):
@@ -616,7 +627,7 @@
         at = pl.multiple_of(part * QT + i * KC, 128)
         s = scores[slot, i]
         top = peak[slot]
-        ps = [jnp.exp2(s[:, c * 128 : (c + 1) * 128] * SCALE - top) for c in range(KC // 128)]
+        ps = [jnp.exp2(s[:, c * 128 : (c + 1) * 128] - top) for c in range(KC // 128)]
         total = ps[0]
         for p in ps[1:]:
             total = total + p
@@ -633,7 +644,6 @@
 def block(x, gain, wq, wk, wv, qd, vd, qu, vu, lengths, tid, slots):
     any_space = pl.BlockSpec(memory_space=pl.ANY)
     smem = pl.BlockSpec(memory_space=pltpu.SMEM)
-    vmem = pl.BlockSpec(memory_space=pltpu.VMEM)
     dma = pltpu.SemaphoreType.DMA
 
     def reduce_scratch(rows):
@@ -648,9 +658,11 @@
     return pl.pallas_call(
         block_kernel,
         out_shape=jax.ShapeDtypeStruct((ROWS, QCOLS), BF16),
-        in_specs=[smem] * 3 + [any_space, vmem] + [any_space] * 7,
-        out_specs=vmem,
+        in_specs=[smem] * 3 + [any_space] * 9,
+        out_specs=any_space,
         scratch_shapes=[
+            pltpu.VMEM((ROWS, QCOLS), BF16),
+            pltpu.VMEM((1, WIDTH), F32),
             pltpu.VMEM((6, ROWS, 256), F32),
             pltpu.VMEM((ROWS, 1024), BF16),
         ]
@@ -678,7 +690,7 @@
         + [
             dma((4,)), dma((8,)), dma((6,)),
             *[dma((COPIES,))] * 4,
-            dma((3,)), dma((3,)), dma((4 * PARTS,)), dma((4 * PARTS,)), *[dma((PARTS,))] * 5,
+            dma((1,)), dma((UNITS,)), dma((3,)), dma((3,)), dma((4 * PARTS,)), dma((4 * PARTS,)), *[dma((PARTS,))] * 5,
             dma((4,)), dma((4,)), dma((4,)), dma((4,)),
         ],
         compiler_params=pltpu.CompilerParams(

time: 69.2 us -> 68.2 us (0.986)
  Pallas kernels: 66.7 us -> 65.5 us
    pallas_call x1, Pallas kernels: 66.7 us -> 65.5 us  [block(): pl.pallas_call(block_kernel, out_shape=jax.ShapeDtypeStruct((ROWS, QCOLS)...]
where the time goes in v5:
time: 68.2 us; the launch traced here: 67.8 us
  Pallas kernels  65.5 us (96%)
  local copies, waits for them, and re-layouts  2.26 us (3%)
    pallas_call x1, Pallas kernels, block(): pl.pallas_call(block_kernel, out_shape=jax.ShapeDtypeStruct((ROWS, QCOLS)...  65.5 us
    unnamed x1, local copies, waits for them, and re-layouts  2.26 us

profile of v5, /device:TPU:1, one launch (start us, length us, event | category | flops | bytes accessed | tf_op | source)
XLA Modules:
  0.0 67.8 jit_solution(17669931517863237532)
XLA Ops:
  0.0 65.5 %block.1 = bf16[512,1024]{1,0:T(8,128)(2,1)} custom-call(s32[16]{0:T(128)} %len_ref.1, s32[16]{0:T(128)} %tid_ref.1, s32[256]{0:T(256)} %table_ref.1, bf16[512,4096]{1,0:T(8,128)(2,1)} %x_hbm.1, f32[1,4096]{1,0:T(1,128)} %bitcast.1, bf16[4096,1024]{1,0:T(8,128)(2,1)} %wq_hbm.1, bf16[4096,256]{1,0:T(8,128)(2,1)} %wk_hbm.1, bf16[4096,256]{1,0:T(8,128)(2,1)} %wv_hbm.1, ...), custom_call_target="tpu_custom_call" | custom-call | tf_op jit(solution)/shard_map/block/pallas_call | solution.py:658
  65.5 2.3 %copy.14 = bf16[512,1024]{1,0:T(8,128)(2,1)} copy(bf16[512,1024]{1,0:T(8,128)(2,1)} %block.1) | data formatting | bytes 2097152

commit v6 on v5

--- a/solution.py
+++ b/solution.py
@@ -391,13 +391,9 @@
 
     def wait_keys():
         for slot in range(2):
-            share(k_win, 0, slot)
-        for slot in range(2):
             share_copy(k_win, 0, slot).wait()
 
     def wait_values():
-        for slot in range(2):
-            share(v_win, 1, slot)
         for slot in range(2):
             share_copy(v_win, 1, slot).wait()
         for c in shrunk_copies():
@@ -414,6 +410,12 @@
 
         def ahead(u, carry):
             score(u, q_own, k_win, q_mark, k_mark, marked, scores, highest, peak)
+            for slot in range(2):
+
+                @pl.when(u == slot)
+                def _(slot=slot):
+                    share(v_win, 1, slot)
+
             return carry
 
         lax.fori_loop(0, AHEAD, ahead, 0)
@@ -518,9 +520,9 @@
             [keys, step(red_d, 1), send_k(0, 1)],
             [values, turn_v(0, 1), send_k(2, 3)],
             [step(red_d, 2), step(red_u, 1), pass_v(0, 1), turn_v(2, 3)],
-            [pass_v(2, 3)],
-            [step(red_d, 3), step(red_u, 2), forward_k(0, 1, 2, 3), after_turn(0, 1)],
-            [forward_v(0, 1), send_v(0, 1, 2, 3), after_turn(2, 3)],
+            [pass_v(2, 3), forward_k(0, 1)],
+            [step(red_d, 3), step(red_u, 2), forward_k(2, 3), after_turn(0, 1)],
+            [forward_v(0, 1), send_v(0, 1, 2, 3), after_turn(2, 3), lambda: share(k_win, 0, 0)],
         ]
 
         def work(j, carry):
@@ -541,6 +543,7 @@
         forward_v(2, 3)()
         shrunk()
         red_u.arrive(4)
+        share(k_win, 0, 1)
         lax.fori_loop(0, 4, query, 0)
 
     pl.run_scoped(

time: 68.2 us -> 66.3 us (0.972)
  Pallas kernels: 65.5 us -> 63.9 us
    pallas_call x1, Pallas kernels: 65.5 us -> 63.9 us  [block(): pl.pallas_call(block_kernel, out_shape=jax.ShapeDtypeStruct((ROWS, QCOLS)...]
where the time goes in v6:
time: 66.3 us; the launch traced here: 66.2 us
  Pallas kernels  63.9 us (96%)
  local copies, waits for them, and re-layouts  2.26 us (3%)
    pallas_call x1, Pallas kernels, block(): pl.pallas_call(block_kernel, out_shape=jax.ShapeDtypeStruct((ROWS, QCOLS)...  63.9 us
    unnamed x1, local copies, waits for them, and re-layouts  2.26 us

profile of v6, /device:TPU:1, one launch (start us, length us, event | category | flops | bytes accessed | tf_op | source)
XLA Modules:
  0.0 66.2 jit_solution(7141532762357715607)
XLA Ops:
  0.0 63.9 %block.1 = bf16[512,1024]{1,0:T(8,128)(2,1)} custom-call(s32[16]{0:T(128)} %len_ref.1, s32[16]{0:T(128)} %tid_ref.1, s32[256]{0:T(256)} %table_ref.1, bf16[512,4096]{1,0:T(8,128)(2,1)} %x_hbm.1, f32[1,4096]{1,0:T(1,128)} %bitcast.1, bf16[4096,1024]{1,0:T(8,128)(2,1)} %wq_hbm.1, bf16[4096,256]{1,0:T(8,128)(2,1)} %wk_hbm.1, bf16[4096,256]{1,0:T(8,128)(2,1)} %wv_hbm.1, ...), custom_call_target="tpu_custom_call" | custom-call | tf_op jit(solution)/shard_map/block/pallas_call | solution.py:661
  63.9 2.3 %copy.14 = bf16[512,1024]{1,0:T(8,128)(2,1)} copy(bf16[512,1024]{1,0:T(8,128)(2,1)} %block.1) | data formatting | bytes 2097152

commit v7 on v6

--- a/solution.py
+++ b/solution.py
@@ -521,7 +521,7 @@
             [values, turn_v(0, 1), send_k(2, 3)],
             [step(red_d, 2), step(red_u, 1), pass_v(0, 1), turn_v(2, 3)],
             [pass_v(2, 3), forward_k(0, 1)],
-            [step(red_d, 3), step(red_u, 2), forward_k(2, 3), after_turn(0, 1)],
+            [step(red_d, 3), forward_k(2, 3), step(red_u, 2), after_turn(0, 1)],
             [forward_v(0, 1), send_v(0, 1, 2, 3), after_turn(2, 3), lambda: share(k_win, 0, 0)],
         ]
 

time: 66.3 us -> 69.4 us (1.047)
  Pallas kernels: 63.9 us -> 66.9 us
    pallas_call x1, Pallas kernels: 63.9 us -> 66.9 us  [block(): pl.pallas_call(block_kernel, out_shape=jax.ShapeDtypeStruct((ROWS, QCOLS)...]
where the time goes in v7:
time: 69.4 us; the launch traced here: 69.2 us
  Pallas kernels  66.9 us (96%)
  local copies, waits for them, and re-layouts  2.26 us (3%)
    pallas_call x1, Pallas kernels, block(): pl.pallas_call(block_kernel, out_shape=jax.ShapeDtypeStruct((ROWS, QCOLS)...  66.9 us
    unnamed x1, local copies, waits for them, and re-layouts  2.26 us

profile of v7, /device:TPU:1, one launch (start us, length us, event | category | flops | bytes accessed | tf_op | source)
XLA Modules:
  0.0 69.2 jit_solution(6197056388685788661)
XLA Ops:
  0.0 66.9 %block.1 = bf16[512,1024]{1,0:T(8,128)(2,1)} custom-call(s32[16]{0:T(128)} %len_ref.1, s32[16]{0:T(128)} %tid_ref.1, s32[256]{0:T(256)} %table_ref.1, bf16[512,4096]{1,0:T(8,128)(2,1)} %x_hbm.1, f32[1,4096]{1,0:T(1,128)} %bitcast.1, bf16[4096,1024]{1,0:T(8,128)(2,1)} %wq_hbm.1, bf16[4096,256]{1,0:T(8,128)(2,1)} %wk_hbm.1, bf16[4096,256]{1,0:T(8,128)(2,1)} %wv_hbm.1, ...), custom_call_target="tpu_custom_call" | custom-call | tf_op jit(solution)/shard_map/block/pallas_call | solution.py:661
  66.9 2.3 %copy.14 = bf16[512,1024]{1,0:T(8,128)(2,1)} copy(bf16[512,1024]{1,0:T(8,128)(2,1)} %block.1) | data formatting | bytes 2097152
